TPU v7x, 512 devices: a whole 4x8x8 slice. The times are simulated.
512 devices in a mesh: lat: 32 (over x, z), lev: 16 (over y, core).
Axes of the slice: x: 4, y: 8, z: 8, core: 2. Of those that a mesh axis runs over, the one named last changes fastest.
Arguments:
- delta_p: float32 [64, 256, 1536], P('lev', 'lat'), may hold values from 0.5 to 1.5
- wind_u: float32 [64, 256, 1536], P('lev', 'lat'), may hold values from -6 to 6
- wind_v: float32 [64, 256, 1536], P('lev', 'lat'), may hold values from -6 to 6
- potential_temp: float32 [64, 256, 1536], P('lev', 'lat'), may hold values from 0.8 to 1.6
- tracer: float32 [64, 256, 1536], P('lev', 'lat'), may hold values from 0 to 1
- courant_north: float32 [64, 256, 1536], P('lev', 'lat'), may hold values from -0.3 to 0.3
- courant_east: float32 [64, 256, 1536], P('lev', 'lat'), may hold values from -0.15 to 0.15
Outputs:
- remapped_dp: float32 [64, 256, 1536], P('lev', 'lat')
- remapped_u: float32 [64, 256, 1536], P('lev', 'lat')
- remapped_v: float32 [64, 256, 1536], P('lev', 'lat')
- remapped_theta: float32 [64, 256, 1536], P('lev', 'lat')
- remapped_tracer: float32 [64, 256, 1536], P('lev', 'lat')
All inputs are finite; a program needn't handle non-finite values.
Results may differ from a plain program's by a relative error of at most 0.0003.
Values sent between devices are 32-bit elements; how exact they have to be, the bound alone decides.
No kernel may reach another device: no remote copies, remote signals or barrier semaphores. Data moves between devices by JAX's collectives and lax.ppermute only.
A program may use at most 64 MiB of HBM per device.

v0:
```python
import jax
import jax.numpy as jnp
from jax import lax
from jax.sharding import PartitionSpec as P

STEPS = 3


ptop_value = 1.0
push_coef = 0.5


def entering(part, axis, combine, identity):
    place = lax.axis_index(axis)
    gathered = lax.all_gather(part, axis)
    state = jnp.zeros_like(part) + jnp.asarray(identity, part.dtype)

    def one(step, state):
        return combine(state, lax.dynamic_index_in_dim(gathered, step, 0, False))

    return lax.fori_loop(0, place, one, state)


def from_behind(x, axis, by):
    size = lax.axis_size(axis)
    pairs = [(i, i + by) for i in range(size) if 0 <= i + by < size]
    return lax.ppermute(x, axis, pairs)


def with_halo(block, sides, width):
    for axis, dim in sides:
        count = lax.axis_size(axis)
        forward = [(i, i + 1) for i in range(count - 1)]
        backward = [(target, source) for source, target in forward]
        low = lax.ppermute(
            lax.slice_in_dim(block, block.shape[dim] - width, None, axis=dim), axis, forward
        )
        high = lax.ppermute(lax.slice_in_dim(block, 0, width, axis=dim), axis, backward)
        block = jnp.concatenate([low, block, high], axis=dim)
    return block


def upwind(speed, upstream_a, upstream_b):
    return jnp.maximum(speed, 0.0) * upstream_a + jnp.minimum(speed, 0.0) * upstream_b


def remap_columns(masses, fields):
    level_count = masses.shape[0]
    layer_top = ptop_value + (jnp.cumsum(masses, axis=0) - masses)
    thickness = jnp.sum(masses, axis=0) / level_count
    target_ids = jnp.arange(1, level_count + 1).astype(jnp.float32)
    targets = ptop_value + target_ids[:, None] * thickness[None, :]
    target_blocks = targets.reshape(level_count // 8, 8, targets.shape[1])

    def cumulate(target_block):
        fraction = jnp.clip((target_block[:, None, :] - layer_top[None]) / masses[None], 0.0, 1.0)
        return jnp.sum(fraction[None] * fields[:, None], axis=2)

    cumulative = lax.map(cumulate, target_blocks)
    cumulative = jnp.moveaxis(cumulative, 1, 0).reshape(
        fields.shape[0], level_count, targets.shape[1]
    )
    shifted = jnp.concatenate([jnp.zeros_like(cumulative[:, :1]), cumulative[:, :-1]], axis=1)
    return (thickness, (cumulative - shifted) / thickness[None, None, :])


def layer_tops(masses):
    column_total = jnp.sum(masses, axis=0)
    before = entering(column_total, "lev", jnp.add, jnp.zeros_like(column_total))
    return ptop_value + before + (jnp.cumsum(masses, axis=0) - masses)


def push_winds(state):
    masses = state[0]
    log_middle = jnp.log(layer_tops(masses) + 0.5 * masses)
    accel = (
        -push_coef
        * state[3]
        * (jnp.roll(log_middle, -1, axis=-1) - jnp.roll(log_middle, 1, axis=-1))
    )
    return jnp.concatenate([state[:1], state[1:2] + accel[None], state[2:]], axis=0)


def transport(padded, north_c, south_c, east_c):
    centre = padded[:, :, 1:-1]
    north_flux = upwind(north_c, centre, padded[:, :, 2:])
    south_flux = upwind(south_c, padded[:, :, :-2], centre)
    east_flux = upwind(east_c, centre, jnp.roll(centre, -1, axis=-1))
    west_flux = jnp.roll(east_flux, 1, axis=-1)
    return centre - (north_flux - south_flux) - (east_flux - west_flux)


def body(delta_p, wind_u, wind_v, potential_temp, tracer, courant_north, courant_east):
    row_count = delta_p.shape[1]
    total_rows = lax.axis_size("lat") * row_count
    global_row = lax.axis_index("lat") * row_count + jnp.arange(row_count, dtype=jnp.int32)
    north_c = jnp.where((global_row < total_rows - 1)[None, :, None], courant_north, 0.0)
    state = jnp.stack(
        [delta_p, wind_u * delta_p, wind_v * delta_p, potential_temp * delta_p, tracer * delta_p]
    )
    below_row = from_behind(north_c[:, -1:, :], "lat", 1)
    south_c = jnp.concatenate([below_row, north_c[:, :-1]], axis=1)
    for sweep_id in range(STEPS):
        state = push_winds(state)
        padded = with_halo(state, (("lat", 2),), 1)
        state = transport(padded, north_c, south_c, courant_east)
    item_block = lax.all_to_all(state, "lev", split_axis=3, concat_axis=1, tiled=True)
    block_shape = item_block.shape
    flat_block = item_block.reshape(block_shape[0], block_shape[1], -1)
    thickness, values = remap_columns(flat_block[0], flat_block[1:])
    filled = jnp.broadcast_to(thickness[None, None], (1, block_shape[1], thickness.shape[0]))
    columns = jnp.concatenate([filled, values], axis=0).reshape(block_shape)
    layers = lax.all_to_all(columns, "lev", split_axis=1, concat_axis=3, tiled=True)
    return (layers[0], layers[1], layers[2], layers[3], layers[4])


def solution(mesh):
    in_specs = (
        P("lev", "lat", None),
        P("lev", "lat", None),
        P("lev", "lat", None),
        P("lev", "lat", None),
        P("lev", "lat", None),
        P("lev", "lat", None),
        P("lev", "lat", None),
    )
    out_specs = (
        P("lev", "lat", None),
        P("lev", "lat", None),
        P("lev", "lat", None),
        P("lev", "lat", None),
        P("lev", "lat", None),
    )
    return jax.shard_map(body, mesh=mesh, in_specs=in_specs, out_specs=out_specs, check_vma=False)
```

profile of v0, /device:TPU:7, one launch (start us, length us, event | category | flops | bytes accessed | tf_op | source)
XLA Modules:
  0.0 289.2 jit_solution(5948086600065179904)
XLA Ops:
  0.6 1.1 copy.419
  1.8 0.9 reduce_sum.45
  2.7 20.3 %all-gather = f32[128,1536]{1,0:T(8,128)S(1)} all-gather(f32[8,1536]{1,0:T(8,128)S(1)} %reduce_sum.45), channel_id=2, replica_groups=mesh['lat'=32,'lev'=16] {'lev'}, dimensions={0}, use_global_device_ids=true | all-gather | bytes 835584 | tf_op jit(solution)/shard_map/all_gather | solution.py:15
  26.0 1.3 fusion.23
  28.0 10.9 %collective-permute-start = (f32[5,4,1,1536]{3,1,2,0:T(4,128)}, f32[5,4,1,1536]{3,1,2,0:T(4,128)S(1)}, u32[]{:S(2)}, u32[]{:S(2)}) collective-permute-start(f32[5,4,1,1536]{3,1,2,0:T(4,128)} %get-tuple-element.175), channel_id=1, source_target_pairs={{16,0},{32,16},{48,32},{64,48},{80,64},{96,80},{112,96},{128,112},... | collective-permute-start | bytes 368648 | tf_op jit(solution)/shard_map/ppermute | solution.py:38
  38.9 1.9 collective-permute-start.2
  41.0 1.9 collective-permute-start.1
  43.3 4.9 %collective-permute-done.1 = f32[4,1,1536]{2,1,0:T(1,128)S(1)} collective-permute-done((f32[4,1,1536]{2,1,0:T(1,128)S(1)}, f32[4,1,1536]{2,1,0:T(1,128)S(1)}, u32[]{:S(2)}, u32[]{:S(2)}) %collective-permute-start.1) | collective-permute-done | bytes 24608 | tf_op jit(solution)/shard_map/ppermute | solution.py:27
  49.9 1.9 fusion.18
  52.0 18.5 %all-gather.1 = f32[128,1536]{1,0:T(8,128)S(1)} all-gather(f32[8,1536]{1,0:T(8,128)S(1)} %get-tuple-element.171), channel_id=3, replica_groups=mesh['lat'=32,'lev'=16] {'lev'}, dimensions={0}, use_global_device_ids=true | all-gather | bytes 835584 | tf_op jit(solution)/shard_map/all_gather | solution.py:15
  72.8 3.6 %collective-permute-start.3 = (f32[5,4,1,1536]{3,1,2,0:T(4,128)S(1)}, f32[5,4,1,1536]{3,1,2,0:T(4,128)S(1)}, u32[]{:S(2)}, u32[]{:S(2)}) collective-permute-start(f32[5,4,1,1536]{3,1,2,0:T(4,128)S(1)} %get-tuple-element.168), channel_id=1, source_target_pairs={{16,0},{32,16},{48,32},{64,48},{80,64},{96,80},{112,96},{128,112},... | collective-permute-start | bytes 368648 | tf_op jit(solution)/shard_map/ppermute | solution.py:38
  76.4 2.1 collective-permute-start.4
  79.4 5.6 %collective-permute-done.4 = f32[5,4,1,1536]{3,1,2,0:T(4,128)S(1)} collective-permute-done((f32[5,4,1,1536]{3,1,2,0:T(4,128)S(1)}, f32[5,4,1,1536]{3,1,2,0:T(4,128)S(1)}, u32[]{:S(2)}, u32[]{:S(2)}) %collective-permute-start.4) | collective-permute-done | bytes 122912 | tf_op jit(solution)/shard_map/ppermute | solution.py:35
  85.1 1.4 fusion.11
  86.6 20.0 %all-gather.2 = f32[128,1536]{1,0:T(8,128)} all-gather(f32[8,1536]{1,0:T(8,128)S(1)} %get-tuple-element.166), channel_id=4, replica_groups=mesh['lat'=32,'lev'=16] {'lev'}, dimensions={0}, use_global_device_ids=true | all-gather | bytes 835584 | tf_op jit(solution)/shard_map/all_gather | solution.py:15
  110.5 0.9 fusion.25
  112.2 1.9 collective-permute-start.5
  114.2 3.5 %collective-permute-start.6 = (f32[5,4,1,1536]{3,1,2,0:T(4,128)S(1)}, f32[5,4,1,1536]{3,1,2,0:T(4,128)S(1)}, u32[]{:S(2)}, u32[]{:S(2)}) collective-permute-start(f32[5,4,1,1536]{3,1,2,0:T(4,128)S(1)} %get-tuple-element.164), channel_id=1, source_target_pairs={{0,16},{16,32},{32,48},{48,64},{64,80},{80,96},{96,112},{112,128},... | collective-permute-start | bytes 368648 | tf_op jit(solution)/shard_map/ppermute | solution.py:35
  119.0 4.0 %collective-permute-done.6 = f32[5,4,1,1536]{3,1,2,0:T(4,128)S(1)} collective-permute-done((f32[5,4,1,1536]{3,1,2,0:T(4,128)S(1)}, f32[5,4,1,1536]{3,1,2,0:T(4,128)S(1)}, u32[]{:S(2)}, u32[]{:S(2)}) %collective-permute-start.6) | collective-permute-done | bytes 122912 | tf_op jit(solution)/shard_map/ppermute | solution.py:35
  123.1 1.4 fusion.4
  124.4 9.6 %copy.453 = f32[5,4,8,1536]{2,1,0,3:T(4,128)} copy(f32[5,4,8,1536]{3,1,2,0:T(4,128)S(1)} %fusion.4) | data formatting | bytes 1966080 | tf_op jit(solution)/shard_map/sub | solution.py:90
  134.0 20.5 %reshape.225 = f32[16,1,15360]{2,1,0:T(1,128)} reshape(f32[1536,5,4,8]{3,2,1,0:T(4,128)} %bitcast.90) | data formatting | bytes 1966080
  154.5 14.4 %all-to-all-start = ((f32[16,1,15360]{2,1,0:T(1,128)}), f32[16,1,15360]{2,1,0:T(1,128)S(1)}, u32[]{:S(2)}, u32[]{:S(2)}) async-start(f32[16,1,15360]{2,1,0:T(1,128)} %reshape.225), calls=%async_computation | async-start | bytes 1966080 | tf_op jit(solution)/shard_map/all_to_all | solution.py:107
  168.9 26.7 %all-to-all-done = f32[16,1,15360]{2,1,0:T(1,128)S(1)} async-done(((f32[16,1,15360]{2,1,0:T(1,128)}), f32[16,1,15360]{2,1,0:T(1,128)S(1)}, u32[]{:S(2)}, u32[]{:S(2)}) %all-to-all-start) | async-done | bytes 983072 | tf_op jit(solution)/shard_map/all_to_all | solution.py:107
  196.1 3.0 %reduce.3 = f32[16,15360]{1,0:T(8,128)S(1)} reduce(f32[16,1,15360]{2,1,0:T(1,128)S(1)} %all-to-all-done, f32[]{:T(128)} %broadcast.117), dimensions={1}, to_apply=%all_to_all.22.reduce_sub_computation | reduce | bytes 1966084 | tf_op jit(solution)/shard_map/all_to_all | solution.py:107
  199.1 24.8 %reshape.226 = f32[1536,5,4,8]{3,2,1,0:T(4,128)} reshape(f32[16,15360]{1,0:T(8,128)S(1)} %reduce.3) | data formatting | bytes 1966080
  223.9 13.0 %copy.454 = f32[5,4,8,16,96]{4,2,1,3,0:T(8,128)S(1)} copy(f32[5,4,8,16,96]{2,1,0,4,3:T(4,128)} %bitcast.91) | data formatting | bytes 1966080 | tf_op jit(solution)/shard_map/all_to_all | solution.py:107
  238.1 0.9 subtract_add_fusion
  239.2 6.7 %while.43 = (s32[]{:T(128)}, f32[8,4,8,768]{3,2,0,1:T(8,128)S(1)}, f32[8,8,768]{2,1,0:T(8,128)S(1)}, f32[64,768]{1,0:T(8,128)S(1)}, f32[1,64,768]{2,1,0:T(8,128)S(1)}, /*index=5*/f32[4,64,768]{2,1,0:T(8,128)S(1)}, s32[]{:T(128)}) while((s32[]{:T(128)}, f32[8,4,8,768]{3,2,0,1:T(8,128)S(1)}, f32[8,8,768]{2,1,0:T(8,128)S(1)}, ...), condition=%wide.region_16.17_spmd, body=%wide.region_14.16_spmd.sunk | while | flops 4300802 | bytes 4694101 | solution.py:59
  246.8 37.2 %all_to_all.30 = f32[5,64,8,96]{3,2,0,1:T(8,128)S(1)} all-to-all(f32[5,64,8,96]{3,2,0,1:T(8,128)S(1)} %copy.456), channel_id=1, replica_groups=mesh['lat'=32,'lev'=16] {'lev'}, dimensions={1} | all-to-all | bytes 1966080 | tf_op jit(solution)/shard_map/all_to_all | solution.py:113
  284.4 0.8 squeeze.41
  288.3 0.8 squeeze.45
  (170 shorter events, 28.3 us)
Async XLA Ops:
  0.6 22.7 %copy-start = (f32[4,8,1536]{2,1,0:T(8,128)S(1)}, f32[4,8,1536]{2,1,0:T(8,128)}, u32[]{:S(2)}) copy-start(f32[4,8,1536]{2,1,0:T(8,128)} %param.15) | copy-start | bytes 589828
  23.0 1.0 copy-start.8
  23.0 1.0 copy-start.9
  23.6 1.0 copy-start.10
  23.8 1.0 copy-start.11
  24.6 0.9 copy-start.12
  25.7 1.6 copy-start.3
  25.8 1.5 copy-start.5
  25.9 14.9 %copy-start.13 = (f32[4,8,1536]{2,1,0:T(8,128)S(1)}, f32[4,8,1536]{2,1,0:T(8,128)}, u32[]{:S(2)}) copy-start(f32[4,8,1536]{2,1,0:T(8,128)} %param.20) | copy-start | bytes 589828
  28.0 20.6 %collective-permute-start = (f32[5,4,1,1536]{3,1,2,0:T(4,128)}, f32[5,4,1,1536]{3,1,2,0:T(4,128)S(1)}, u32[]{:S(2)}, u32[]{:S(2)}) collective-permute-start(f32[5,4,1,1536]{3,1,2,0:T(4,128)} %get-tuple-element.175), channel_id=1, source_target_pairs={{16,0},{32,16},{48,32},{64,48},{80,64},{96,80},{112,96},{128,112},... | collective-permute-start | bytes 368648 | tf_op jit(solution)/shard_map/ppermute | solution.py:38
  38.9 9.7 %collective-permute-start.2 = (f32[5,4,1,1536]{3,1,2,0:T(4,128)S(1)}, f32[5,4,1,1536]{3,1,2,0:T(4,128)S(1)}, u32[]{:S(2)}, u32[]{:S(2)}) collective-permute-start(f32[5,4,1,1536]{3,1,2,0:T(4,128)S(1)} %get-tuple-element.176), channel_id=1, source_target_pairs={{0,16},{16,32},{32,48},{48,64},{64,80},{80,96},{96,112},{112,128},... | collective-permute-start | bytes 368648 | tf_op jit(solution)/shard_map/ppermute | solution.py:35
  41.0 7.2 %collective-permute-start.1 = (f32[4,1,1536]{2,1,0:T(1,128)S(1)}, f32[4,1,1536]{2,1,0:T(1,128)S(1)}, u32[]{:S(2)}, u32[]{:S(2)}) collective-permute-start(f32[4,1,1536]{2,1,0:T(1,128)S(1)} %slice.250), channel_id=1, source_target_pairs={{0,16},{16,32},{32,48},{48,64},{64,80},{80,96},{96,112},{112,128},... | collective-permute-start | bytes 73736 | tf_op jit(solution)/shard_map/ppermute | solution.py:27
  48.6 3.3 %copy-start.1 = (f32[4,8,1536]{2,0,1:T(4,128)}, f32[4,8,1536]{2,0,1:T(4,128)S(1)}, u32[]{:S(2)}) copy-start(f32[4,8,1536]{2,0,1:T(4,128)S(1)} %copy.434) | copy-start | bytes 589828
  48.6 0.7 copy-start.14
  49.3 0.6 copy-start.15
  72.1 6.4 %copy-start.4 = (f32[4,8,1536]{2,0,1:T(4,128)S(1)}, f32[4,8,1536]{2,0,1:T(4,128)}, u32[]{:S(2)}) copy-start(f32[4,8,1536]{2,0,1:T(4,128)} %copy-done.3) | copy-start | bytes 589828
  72.2 6.4 %copy-start.6 = (f32[4,8,1536]{2,0,1:T(4,128)S(1)}, f32[4,8,1536]{2,0,1:T(4,128)}, u32[]{:S(2)}) copy-start(f32[4,8,1536]{2,0,1:T(4,128)} %copy-done.5) | copy-start | bytes 589828
  72.8 6.6 %collective-permute-start.3 = (f32[5,4,1,1536]{3,1,2,0:T(4,128)S(1)}, f32[5,4,1,1536]{3,1,2,0:T(4,128)S(1)}, u32[]{:S(2)}, u32[]{:S(2)}) collective-permute-start(f32[5,4,1,1536]{3,1,2,0:T(4,128)S(1)} %get-tuple-element.168), channel_id=1, source_target_pairs={{16,0},{32,16},{48,32},{64,48},{80,64},{96,80},{112,96},{128,112},... | collective-permute-start | bytes 368648 | tf_op jit(solution)/shard_map/ppermute | solution.py:38
  76.4 8.6 %copy-start.2 = (f32[4,8,1536]{2,0,1:T(4,128)S(1)}, f32[4,8,1536]{2,0,1:T(4,128)}, u32[]{:S(2)}) copy-start(f32[4,8,1536]{2,0,1:T(4,128)} %copy-done.1) | copy-start | bytes 589828
  76.4 8.6 %collective-permute-start.4 = (f32[5,4,1,1536]{3,1,2,0:T(4,128)S(1)}, f32[5,4,1,1536]{3,1,2,0:T(4,128)S(1)}, u32[]{:S(2)}, u32[]{:S(2)}) collective-permute-start(f32[5,4,1,1536]{3,1,2,0:T(4,128)S(1)} %get-tuple-element.169), channel_id=1, source_target_pairs={{0,16},{16,32},{32,48},{48,64},{64,80},{80,96},{96,112},{112,128},... | collective-permute-start | bytes 368648 | tf_op jit(solution)/shard_map/ppermute | solution.py:35
  112.2 6.8 %collective-permute-start.5 = (f32[5,4,1,1536]{3,1,2,0:T(4,128)S(1)}, f32[5,4,1,1536]{3,1,2,0:T(4,128)S(1)}, u32[]{:S(2)}, u32[]{:S(2)}) collective-permute-start(f32[5,4,1,1536]{3,1,2,0:T(4,128)S(1)} %get-tuple-element.163), channel_id=1, source_target_pairs={{16,0},{32,16},{48,32},{64,48},{80,64},{96,80},{112,96},{128,112},... | collective-permute-start | bytes 368648 | tf_op jit(solution)/shard_map/ppermute | solution.py:38
  114.2 8.9 %collective-permute-start.6 = (f32[5,4,1,1536]{3,1,2,0:T(4,128)S(1)}, f32[5,4,1,1536]{3,1,2,0:T(4,128)S(1)}, u32[]{:S(2)}, u32[]{:S(2)}) collective-permute-start(f32[5,4,1,1536]{3,1,2,0:T(4,128)S(1)} %get-tuple-element.164), channel_id=1, source_target_pairs={{0,16},{16,32},{32,48},{48,64},{64,80},{80,96},{96,112},{112,128},... | collective-permute-start | bytes 368648 | tf_op jit(solution)/shard_map/ppermute | solution.py:35
  154.5 41.1 %all-to-all-start = ((f32[16,1,15360]{2,1,0:T(1,128)}), f32[16,1,15360]{2,1,0:T(1,128)S(1)}, u32[]{:S(2)}, u32[]{:S(2)}) async-start(f32[16,1,15360]{2,1,0:T(1,128)} %reshape.225), calls=%async_computation | async-start | bytes 1966080 | tf_op jit(solution)/shard_map/all_to_all | solution.py:107
  237.2 0.7 copy-start.7
where the time goes:
time: 291 us; the launch traced here: 289 us
  blocking collectives  96 us (33%)
  local copies, waits for them, and re-layouts  85.8 us (29%)
  waiting for transfers between devices  42.2 us (15%)
  starting transfers between devices  40.3 us (14%)
  other arithmetic  23 us (8%)
    all_gather x3, blocking collectives, entering(): gathered = lax.all_gather(part, axis)  58.8 us
    unnamed x36, local copies, waits for them, and re-layouts  49 us
    all_to_all x1, blocking collectives, body(): lax.all_to_all(columns, 'lev', split_axis=1, concat_axis=3, tiled=True)  37.2 us
    all_to_all x1, waiting for transfers between devices, body(): lax.all_to_all(state, 'lev', split_axis=3, concat_axis=1, tiled=True)  26.7 us
    ppermute x3, starting transfers between devices, with_halo(): lax.ppermute(lax.slice_in_dim(block, 0, width, axis=dim), axis, backward)  16.5 us
    all_to_all x1, starting transfers between devices, body(): lax.all_to_all(state, 'lev', split_axis=3, concat_axis=1, tiled=True)  14.4 us
    all_to_all x2, local copies, waits for them, and re-layouts, body(): lax.all_to_all(state, 'lev', split_axis=3, concat_axis=1, tiled=True)  13.5 us
    ppermute x3, waiting for transfers between devices, with_halo(): lax.ppermute(lax.slice_in_dim(block, block.shape[dim] - width, None, axis...  9.66 us
  transfers between devices with their start and end apart: 8, of which 6 were waited for; matrix products, arithmetic and copies ran while one was open for 1% of the time, Pallas kernels for 0%

commit v1 on v0

v1 whole, which is shorter than its diff:
```python
import functools

import jax
import jax.numpy as jnp
from jax import lax
from jax.experimental import pallas as pl
from jax.experimental.pallas import tpu as pltpu
from jax.sharding import PartitionSpec as P

STEPS = 3
LEVELS = 64
OWN = 4
GROUP = 16
WIDTH = 96
LANES = 128
TILES = 12
FIELDS = 5
CARRIED = 7
VMEM = pltpu.VMEM


def lane_ids():
    return lax.broadcasted_iota(jnp.int32, (8, LANES), 1)


def row_ids():
    return lax.broadcasted_iota(jnp.int32, (8, LANES), 0)


def pack_kernel(last_ref, dp_ref, u_ref, v_ref, th_ref, tr_ref, cn_ref, ce_ref, out_ref):
    lane = lane_ids()
    closed = jnp.logical_and(last_ref[0] > 0, row_ids() == 7)

    def level(l, _):
        for field, ref in enumerate((dp_ref, u_ref, v_ref, th_ref, tr_ref, cn_ref, ce_ref)):
            tiles = []
            for t in range(TILES):
                x = ref[l, :, t * LANES : (t + 1) * LANES]
                if 1 <= field <= 4:
                    x = x * dp_ref[l, :, t * LANES : (t + 1) * LANES]
                if field == 5:
                    x = jnp.where(closed, 0.0, x)
                tiles.append(x)
            for d in range(GROUP):
                first = d * WIDTH - 16
                a, off = first // LANES, first % LANES
                x = jnp.where(lane >= off, tiles[a % TILES], tiles[(a + 1) % TILES])
                out_ref[d, field * OWN + l] = x
        return 0

    lax.fori_loop(0, OWN, level, 0)


def pack(last, args):
    return pl.pallas_call(
        pack_kernel,
        out_shape=jax.ShapeDtypeStruct((GROUP, CARRIED * OWN, 8, LANES), jnp.float32),
        in_specs=[pl.BlockSpec(memory_space=pltpu.SMEM)] + [pl.BlockSpec(memory_space=VMEM)] * 7,
        out_specs=pl.BlockSpec(memory_space=VMEM),
        name="pack",
    )(last, *args)


def edges_kernel(x_ref, north_ref, south_ref):
    def group(g, _):
        for i in range(8):
            for f in range(CARRIED):
                at = (2 * g + i // OWN, f * OWN + i % OWN)
                north_ref[f, g, 3 * i : 3 * i + 3, :] = x_ref[at[0], at[1], 5:8, :]
                south_ref[f, g, 3 * i : 3 * i + 3, :] = x_ref[at[0], at[1], 0:3, :]
        return 0

    lax.fori_loop(0, 8, group, 0)


def edges(x):
    shape = jax.ShapeDtypeStruct((CARRIED, 8, 24, LANES), jnp.float32)
    return pl.pallas_call(
        edges_kernel,
        out_shape=(shape, shape),
        in_specs=[pl.BlockSpec(memory_space=VMEM)],
        out_specs=(pl.BlockSpec(memory_space=VMEM),) * 2,
        name="edges",
    )(x)


def up(pair, is_top):
    m, h = (pltpu.roll(x, 7, 0) for x in pair)
    return jnp.where(is_top, h, m), jnp.where(is_top, m, h)


def down(pair, is_bottom):
    m, h = (pltpu.roll(x, 1, 0) for x in pair)
    return jnp.where(is_bottom, h, m), jnp.where(is_bottom, m, h)


def advance_pair(x, cn, ce, masks, both):
    is_top, is_bottom = masks
    nxt = up(x, is_top)
    north = tuple(cn[0][p] * x[p] + cn[1][p] * nxt[p] for p in range(2))
    south = down(north, is_bottom)
    out = []
    for p in range(2 if both else 1):
        east = ce[0][p] * x[p] + ce[1][p] * pltpu.roll(x[p], LANES - 1, 1)
        west = pltpu.roll(east, 1, 1)
        out.append(x[p] - (north[p] - south[p]) - (east - west))
    return tuple(out)


def columns_kernel(x_ref, north_ref, south_ref, out_ref, halo, top, inverse, final):
    is_top, is_bottom = row_ids() == 7, row_ids() == 0
    masks = (is_top, is_bottom)
    halo[...] = jnp.zeros_like(halo)

    def group(g, runs):
        runs = list(runs)
        for i in range(8):
            for f in range(CARRIED):
                halo[f, i, 0:3, :] = north_ref[f, g, 3 * i : 3 * i + 3, :]
                halo[f, i, 5:8, :] = south_ref[f, g, 3 * i : 3 * i + 3, :]
        for i in range(8):
            state = [(x_ref[2 * g + i // OWN, f * OWN + i % OWN], halo[f, i]) for f in range(CARRIED)]
            cn, ce = (
                (tuple(jnp.maximum(c, 0.0) for c in pair), tuple(jnp.minimum(c, 0.0) for c in pair))
                for pair in state[FIELDS:]
            )
            state = state[:FIELDS]
            for step in range(STEPS):
                pushed = []
                for p in range(2):
                    run = runs[2 * step + p]
                    mass = state[0][p]
                    log_middle = jnp.log(run + 0.5 * mass)
                    slope = pltpu.roll(log_middle, LANES - 1, 1) - pltpu.roll(log_middle, 1, 1)
                    pushed.append(state[1][p] - 0.5 * state[3][p] * slope)
                    runs[2 * step + p] = run + mass
                state[1] = tuple(pushed)
                state = [advance_pair(x, cn, ce, masks, step < STEPS - 1) for x in state]
            at = 8 * g + i
            mass = state[0][0]
            top[at] = runs[-1]
            runs[-1] = runs[-1] + mass
            inverse[at] = 1.0 / mass
            for f in range(1, FIELDS):
                final[f - 1, at] = state[f][0]
        return tuple(runs)

    one = jnp.ones((8, LANES), jnp.float32)
    runs = lax.fori_loop(0, 8, group, (one,) * (2 * STEPS + 1))
    h = (runs[-1] - 1.0) * (1.0 / LEVELS)
    inverse_h = 1.0 / h

    def targets(kb, last):
        base = 1.0 + h * (8 * kb + 1).astype(jnp.float32)

        def layer(j, acc):
            inv = inverse[j]
            u = (base - top[j]) * inv
            stride = h * inv
            values = [final[f, j] for f in range(4)]
            acc = list(acc)
            for k in range(8):
                w = jnp.minimum(jnp.maximum(u, 0.0), 1.0)
                for f in range(4):
                    acc[4 * k + f] = acc[4 * k + f] + w * values[f]
                if k < 7:
                    u = u + stride
            return tuple(acc)

        acc = lax.fori_loop(0, LEVELS, layer, (jnp.zeros((8, LANES), jnp.float32),) * 32)
        for k in range(8):
            for f in range(4):
                below = acc[4 * (k - 1) + f] if k else last[f]
                out_ref[2 * kb + k // OWN, f * OWN + k % OWN] = (acc[4 * k + f] - below) * inverse_h
        return tuple(acc[28:])

    lax.fori_loop(0, 8, targets, (jnp.zeros((8, LANES), jnp.float32),) * 4)
    for d in range(GROUP):
        out_ref[d, 16] = h


def columns(x, north, south):
    return pl.pallas_call(
        columns_kernel,
        out_shape=jax.ShapeDtypeStruct((GROUP, 17, 8, LANES), jnp.float32),
        in_specs=[pl.BlockSpec(memory_space=VMEM)] * 3,
        out_specs=pl.BlockSpec(memory_space=VMEM),
        scratch_shapes=[
            VMEM((CARRIED, 8, 8, LANES), jnp.float32),
            VMEM((LEVELS, 8, LANES), jnp.float32),
            VMEM((LEVELS, 8, LANES), jnp.float32),
            VMEM((4, LEVELS, 8, LANES), jnp.float32),
        ],
        name="columns",
    )(x, north, south)


def unpack_kernel(x_ref, dp_ref, u_ref, v_ref, th_ref, tr_ref):
    lane = lane_ids()

    def merged(t, at):
        first = 4 * t // 3
        edge = (first + 1) * WIDTH - t * LANES
        if edge >= LANES:
            return x_ref[first, at]
        return jnp.where(lane < edge, x_ref[first, at], x_ref[first + 1, at])

    for t in range(TILES):
        span = slice(t * LANES, (t + 1) * LANES)
        h = merged(t, 16)
        for l in range(OWN):
            dp_ref[l, :, span] = h
            for f, ref in enumerate((u_ref, v_ref, th_ref, tr_ref)):
                ref[l, :, span] = merged(t, f * OWN + l)


def unpack(x):
    shape = jax.ShapeDtypeStruct((OWN, 8, TILES * LANES), jnp.float32)
    return pl.pallas_call(
        unpack_kernel,
        out_shape=(shape,) * 5,
        in_specs=[pl.BlockSpec(memory_space=VMEM)],
        out_specs=(pl.BlockSpec(memory_space=VMEM),) * 5,
        name="unpack",
    )(x)


def body(*args):
    lats = lax.axis_size("lat")
    last = (lax.axis_index("lat") == lats - 1).astype(jnp.int32).reshape(1)
    sent = pack(last, args)
    held = lax.all_to_all(sent, "lev", 0, 0, tiled=True)
    to_north, to_south = edges(held)
    forward = [(i, i + 1) for i in range(lats - 1)]
    backward = [(b, a) for a, b in forward]
    south = lax.ppermute(to_north, "lat", forward)
    north = lax.ppermute(to_south, "lat", backward)
    made = columns(held, north, south)
    back = lax.all_to_all(made, "lev", 0, 0, tiled=True)
    return tuple(unpack(back))


def solution(mesh):
    spec = P("lev", "lat", None)
    return jax.shard_map(body, mesh=mesh, in_specs=(spec,) * 7, out_specs=(spec,) * 5, check_vma=False)
```

time: 291 us -> 157 us (0.54)
  local copies, waits for them, and re-layouts: 85.8 us -> 0.85 us
  Pallas kernels: 0 us -> 34.8 us
  starting transfers between devices: 40.3 us -> 12.8 us
  other arithmetic: 23 us -> 0 us
  waiting for transfers between devices: 42.2 us -> 19.4 us
  blocking collectives: 96 us -> 88.4 us
    all_gather x3 -> x0, blocking collectives: 58.8 us -> none  [entering(): gathered = lax.all_gather(part, axis)]
    all_to_all x1 -> x2, blocking collectives: 37.2 us -> 88.4 us  [the longest x1 53.2 us: body(): held = lax.all_to_all(sent, 'lev', 0, 0, tiled=True)]
    unnamed x36 -> x4, local copies, waits for them, and re-layouts: 49 us -> 0.85 us
    pallas_call x0 -> x4, Pallas kernels: none -> 34.8 us  [the longest x1 26.7 us: columns(): pl.pallas_call(columns_kernel, out_shape=jax.ShapeDtypeStruct((GROUP, 17,...]
    all_to_all x1 -> x0, waiting for transfers between devices: 26.7 us -> none  [body(): lax.all_to_all(state, 'lev', split_axis=3, concat_axis=1, tiled=True)]
    all_to_all x1 -> x0, starting transfers between devices: 14.4 us -> none  [body(): lax.all_to_all(state, 'lev', split_axis=3, concat_axis=1, tiled=True)]
    all_to_all x3 -> x0, local copies, waits for them, and re-layouts: 13.6 us -> none  [the longest x2 13.5 us: body(): lax.all_to_all(state, 'lev', split_axis=3, concat_axis=1, tiled=True)]
    ppermute x7 -> x2, starting transfers between devices: 25.9 us -> 12.8 us  [the longest x1 10.9 us: body(): north = lax.ppermute(to_south, 'lat', backward)]
  transfers between devices with their start and end apart: 8 -> 2, of which waited for: 6 -> 2; matrix products, arithmetic and copies ran while one was open for 1% -> 0% of each run, Pallas kernels for 0% -> 0%
where the time goes in v1:
time: 157 us
  blocking collectives  88.4 us (56%)
  Pallas kernels  34.8 us (22%)
  waiting for transfers between devices  19.4 us (12%)
  starting transfers between devices  12.8 us (8%)
    all_to_all x1, blocking collectives, body(): held = lax.all_to_all(sent, 'lev', 0, 0, tiled=True)  53.2 us
    all_to_all x1, blocking collectives, body(): back = lax.all_to_all(made, 'lev', 0, 0, tiled=True)  35.3 us
    pallas_call x1, Pallas kernels, columns(): pl.pallas_call(columns_kernel, out_shape=jax.ShapeDtypeStruct((GROUP, 17,...  26.7 us
    ppermute x1, waiting for transfers between devices, body(): north = lax.ppermute(to_south, 'lat', backward)  13.5 us
    ppermute x1, starting transfers between devices, body(): north = lax.ppermute(to_south, 'lat', backward)  10.9 us
    ppermute x1, waiting for transfers between devices, body(): south = lax.ppermute(to_north, 'lat', forward)  5.84 us
  transfers between devices with their start and end apart: 2, of which 2 were waited for; matrix products, arithmetic and copies ran while one was open for 0% of the time, Pallas kernels for 0%

profile of v1, /device:TPU:7, one launch (start us, length us, event | category | flops | bytes accessed | tf_op | source)
XLA Modules:
  0.0 157.0 jit_solution(15329032124211281909)
XLA Ops:
  0.6 2.9 %pack.1 = f32[16,28,8,128]{3,2,1,0:T(8,128)} custom-call(s32[1]{0:T(128)} %bitcast.last_ref, f32[4,8,1536]{2,1,0:T(8,128)} %dp_ref.1, f32[4,8,1536]{2,1,0:T(8,128)} %u_ref.1, f32[4,8,1536]{2,1,0:T(8,128)} %v_ref.1, f32[4,8,1536]{2,1,0:T(8,128)} %th_ref.1, f32[4,8,1536]{2,1,0:T(8,128)} %tr_ref.1, f32[4,8,1536]{2,1,0:T(8,128)} %cn_ref.1, f32[4,8,1536]{2,1,0:T(8,128)} %ce_ref.1), custom_call_target="tpu_custom_call" | custom-call | tf_op jit(solution)/shard_map/pack/pallas_call | solution.py:55
  3.5 53.2 %all_to_all.10.x_ref = f32[16,28,8,128]{3,2,1,0:T(8,128)} all-to-all(f32[16,28,8,128]{3,2,1,0:T(8,128)} %pack.1), channel_id=1, replica_groups=mesh['lat'=32,'lev'=16] {'lev'}, dimensions={0} | all-to-all | bytes 3670016 | tf_op jit(solution)/shard_map/all_to_all | solution.py:232
  56.7 3.1 %edges.1 = (f32[7,8,24,128]{3,2,1,0:T(8,128)}, f32[7,8,24,128]{3,2,1,0:T(8,128)}) custom-call(f32[16,28,8,128]{3,2,1,0:T(8,128)} %all_to_all.10.x_ref), custom_call_target="tpu_custom_call" | custom-call | tf_op jit(solution)/shard_map/edges/pallas_call | solution.py:78
  59.8 10.9 %collective-permute-start = (f32[7,8,24,128]{3,2,1,0:T(8,128)}, f32[7,8,24,128]{3,2,1,0:T(8,128)S(1)}, u32[]{:S(2)}, u32[]{:S(2)}) collective-permute-start(f32[7,8,24,128]{3,2,1,0:T(8,128)} %get-tuple-element.7), channel_id=1, source_target_pairs={{16,0},{32,16},{48,32},{64,48},{80,64},{96,80},{112,96},{128,112},... | collective-permute-start | bytes 2064392 | tf_op jit(solution)/shard_map/ppermute | solution.py:237
  70.7 1.9 %collective-permute-start.1 = (f32[7,8,24,128]{3,2,1,0:T(8,128)}, f32[7,8,24,128]{3,2,1,0:T(8,128)S(1)}, u32[]{:S(2)}, u32[]{:S(2)}) collective-permute-start(f32[7,8,24,128]{3,2,1,0:T(8,128)} %get-tuple-element.8), channel_id=1, source_target_pairs={{0,16},{16,32},{32,48},{48,64},{64,80},{80,96},{96,112},{112,128},... | collective-permute-start | bytes 2064392 | tf_op jit(solution)/shard_map/ppermute | solution.py:236
  72.6 13.5 %collective-permute-done.north_ref = f32[7,8,24,128]{3,2,1,0:T(8,128)S(1)} collective-permute-done((f32[7,8,24,128]{3,2,1,0:T(8,128)}, f32[7,8,24,128]{3,2,1,0:T(8,128)S(1)}, u32[]{:S(2)}, u32[]{:S(2)}) %collective-permute-start) | collective-permute-done | bytes 688160 | tf_op jit(solution)/shard_map/ppermute | solution.py:237
  86.1 0.0 copy-start
  86.1 5.8 %collective-permute-done.1.south_ref = f32[7,8,24,128]{3,2,1,0:T(8,128)S(1)} collective-permute-done((f32[7,8,24,128]{3,2,1,0:T(8,128)}, f32[7,8,24,128]{3,2,1,0:T(8,128)S(1)}, u32[]{:S(2)}, u32[]{:S(2)}) %collective-permute-start.1) | collective-permute-done | bytes 688160 | tf_op jit(solution)/shard_map/ppermute | solution.py:236
  92.0 0.0 copy-done
  92.0 0.0 copy-start.1
  92.0 0.8 copy-done.1
  92.8 26.7 %columns.1 = f32[16,17,8,128]{3,2,1,0:T(8,128)} custom-call(f32[16,28,8,128]{3,2,1,0:T(8,128)} %all_to_all.10.x_ref, f32[7,8,24,128]{3,2,1,0:T(8,128)} %copy-done, f32[7,8,24,128]{3,2,1,0:T(8,128)} %copy-done.1), custom_call_target="tpu_custom_call" | custom-call | tf_op jit(solution)/shard_map/columns/pallas_call | solution.py:183
  119.5 35.3 %all_to_all.11.x_ref = f32[16,17,8,128]{3,2,1,0:T(8,128)} all-to-all(f32[16,17,8,128]{3,2,1,0:T(8,128)} %columns.1), channel_id=1, replica_groups=mesh['lat'=32,'lev'=16] {'lev'}, dimensions={0} | all-to-all | bytes 2228224 | tf_op jit(solution)/shard_map/all_to_all | solution.py:239
  154.8 2.2 %unpack.1 = (f32[4,8,1536]{2,1,0:T(8,128)}, f32[4,8,1536]{2,1,0:T(8,128)}, f32[4,8,1536]{2,1,0:T(8,128)}, f32[4,8,1536]{2,1,0:T(8,128)}, f32[4,8,1536]{2,1,0:T(8,128)}) custom-call(f32[16,17,8,128]{3,2,1,0:T(8,128)} %all_to_all.11.x_ref), custom_call_target="tpu_custom_call" | custom-call | tf_op jit(solution)/shard_map/unpack/pallas_call | solution.py:219
Async XLA Ops:
  59.8 26.4 %collective-permute-start = (f32[7,8,24,128]{3,2,1,0:T(8,128)}, f32[7,8,24,128]{3,2,1,0:T(8,128)S(1)}, u32[]{:S(2)}, u32[]{:S(2)}) collective-permute-start(f32[7,8,24,128]{3,2,1,0:T(8,128)} %get-tuple-element.7), channel_id=1, source_target_pairs={{16,0},{32,16},{48,32},{64,48},{80,64},{96,80},{112,96},{128,112},... | collective-permute-start | bytes 2064392 | tf_op jit(solution)/shard_map/ppermute | solution.py:237
  70.7 21.3 %collective-permute-start.1 = (f32[7,8,24,128]{3,2,1,0:T(8,128)}, f32[7,8,24,128]{3,2,1,0:T(8,128)S(1)}, u32[]{:S(2)}, u32[]{:S(2)}) collective-permute-start(f32[7,8,24,128]{3,2,1,0:T(8,128)} %get-tuple-element.8), channel_id=1, source_target_pairs={{0,16},{16,32},{32,48},{48,64},{64,80},{80,96},{96,112},{112,128},... | collective-permute-start | bytes 2064392 | tf_op jit(solution)/shard_map/ppermute | solution.py:236
  86.1 5.8 %copy-start = (f32[7,8,24,128]{3,2,1,0:T(8,128)}, f32[7,8,24,128]{3,2,1,0:T(8,128)S(1)}, u32[]{:S(2)}) copy-start(f32[7,8,24,128]{3,2,1,0:T(8,128)S(1)} %collective-permute-done.north_ref) | copy-start | bytes 2064388
  92.0 0.8 copy-start.1

commit v2 on v0

v2 whole, which is shorter than its diff:
```python
import functools

import jax
import jax.numpy as jnp
from jax import lax
from jax.experimental import pallas as pl
from jax.experimental.pallas import tpu as pltpu
from jax.sharding import PartitionSpec as P

STEPS = 3
LEVELS = 64
OWN = 4
GROUP = 16
WIDTH = 96
SPARE = 32
LANES = 128
TILES = 12
ROWS = 8
VMEM, SMEM = pltpu.VMEM, pltpu.SMEM

CHUNK_A = ((4, 4), (3, 3), (3, 3), (3, 4))
CHUNK_B = ((3, 3), (3, 3), (3, 3))


def places(chunk):
    at, out = 0, []
    for east, west in chunk:
        out.append([])
        for _ in range(OWN):
            out[-1].append((at, at + east))
            at += east + west
    assert at <= LANES
    return out


def tile_count(chunk):
    return 3 * len(chunk) + 1


def turn(x, by):
    by %= LANES
    return pltpu.roll(x, by, 1) if by else x


def iota(axis):
    return lax.broadcasted_iota(jnp.int32, (ROWS, LANES), axis)


def vmem(*shape):
    return jax.ShapeDtypeStruct(shape + (ROWS, LANES), jnp.float32)


IN_VMEM = pl.BlockSpec(memory_space=VMEM)
IN_SMEM = pl.BlockSpec(memory_space=SMEM)


def pack_kernel(last_ref, dp_ref, u_ref, v_ref, th_ref, tr_ref, cn_ref, ce_ref, a_ref, b_ref):
    lane = iota(1)
    closed = jnp.logical_and(last_ref[0] > 0, iota(0) == ROWS - 1)

    def load(ref, l, t):
        x = ref[l, :, t * LANES : (t + 1) * LANES]
        if any(ref is other for other in (u_ref, v_ref, th_ref, tr_ref)):
            x = x * dp_ref[l, :, t * LANES : (t + 1) * LANES]
        if ref is cn_ref:
            x = jnp.where(closed, 0.0, x)
        return x

    for chunk, refs, out_ref in (
        (CHUNK_A, (dp_ref, th_ref, cn_ref, ce_ref), a_ref),
        (CHUNK_B, (u_ref, v_ref, tr_ref), b_ref),
    ):
        where = places(chunk)
        for d in range(GROUP):
            gap = (3 * d + 3) % 4
            first = d * WIDTH - 16
            a, off = (first // LANES) % TILES, first % LANES
            slot = lane // SPARE
            rel = (lane - gap * SPARE) % LANES
            sides = jnp.zeros((ROWS, LANES), jnp.float32)
            for f, ref in enumerate(refs):
                east, west = chunk[f]
                own = []
                for l in range(OWN):
                    x = jnp.where(lane >= off, load(ref, l, a), load(ref, l, (a + 1) % TILES))
                    at_east, at_west = where[f][l]
                    sides = jnp.where(rel >= at_east, turn(x, at_east), sides)
                    sides = jnp.where(rel >= at_west, turn(x, at_west - (SPARE - west)), sides)
                    own.append(x)
                for i in range(3):
                    out_ref[d, 3 * f + i] = jnp.where(slot == gap, turn(own[3], -SPARE * (1 + i)), own[i])
            out_ref[d, 3 * len(chunk)] = sides


def pack(last, args):
    return pl.pallas_call(
        pack_kernel,
        out_shape=(vmem(GROUP, tile_count(CHUNK_A)), vmem(GROUP, tile_count(CHUNK_B))),
        in_specs=[IN_SMEM] + [IN_VMEM] * 7,
        out_specs=(IN_VMEM,) * 2,
        name="pack",
    )(last, *args)


def edges_kernel(chunk, outs, gap_ref, x_ref, *refs):
    north_ref, south_ref = refs[-2:]
    out_refs = [ref.at[k] for ref, n in zip(refs[:-2], outs) for k in range(n)]
    where = places(chunk)
    gap = gap_ref[0]
    rel = (iota(1) - gap * SPARE + LANES) % LANES
    quarter = rel // SPARE

    def group(g, _):
        for half in range(2):
            src = 2 * g + half
            sides = x_ref[src, 3 * len(chunk)]
            for f, (east, west) in enumerate(chunk):
                t = [x_ref[src, 3 * f + i] for i in range(3)]
                fourth = jnp.where(
                    quarter == 1,
                    turn(t[0], SPARE),
                    jnp.where(quarter == 2, turn(t[1], 2 * SPARE), turn(t[2], 3 * SPARE)),
                )
                for l, x in enumerate(t + [fourth]):
                    at_east, at_west = where[f][l]
                    x = jnp.where(quarter == 0, 0.0, x)
                    x = jnp.where(rel < east, turn(sides, -at_east), x)
                    in_west = jnp.logical_and(rel >= SPARE - west, rel < SPARE)
                    x = jnp.where(in_west, turn(sides, SPARE - west - at_west), x)
                    i = OWN * half + l
                    out_refs[f][OWN * src + l] = x
                    north_ref[f, g, 3 * i : 3 * i + 3, :] = x[5:8]
                    south_ref[f, g, 3 * i : 3 * i + 3, :] = x[0:3]
        return 0

    lax.fori_loop(0, 8, group, 0)


def edges(chunk, outs, gap, x):
    strip = jax.ShapeDtypeStruct((len(chunk), 8, 24, LANES), jnp.float32)
    return pl.pallas_call(
        functools.partial(edges_kernel, chunk, outs),
        out_shape=tuple(vmem(n, LEVELS) for n in outs) + (strip, strip),
        in_specs=[IN_SMEM, IN_VMEM],
        out_specs=(IN_VMEM,) * (len(outs) + 2),
        name="edges",
    )(gap, x)


def join_strips(north_ref, south_ref, halo_refs):
    for f, halo in enumerate(halo_refs):
        halo[...] = jnp.zeros(halo.shape, jnp.float32)

    def group(g, _):
        for f, halo in enumerate(halo_refs):
            for i in range(8):
                halo[8 * g + i, 0:3, :] = north_ref[f, g, 3 * i : 3 * i + 3, :]
                halo[8 * g + i, 5:8, :] = south_ref[f, g, 3 * i : 3 * i + 3, :]
        return 0

    lax.fori_loop(0, 8, group, 0)


def shifted(pair, by, edge):
    m, h = (pltpu.roll(x, by, 0) for x in pair)
    return jnp.where(edge, h, m), jnp.where(edge, m, h)


def coefficients(cn, ce, is_top, is_bottom):
    cs = shifted(cn, 1, is_bottom)
    out = []
    for p in range(2):
        cw = pltpu.roll(ce[p], 1, 1)
        south, west = jnp.maximum(cs[p], 0.0), jnp.maximum(cw, 0.0)
        north, east = jnp.maximum(-cn[p], 0.0), jnp.maximum(-ce[p], 0.0)
        own = 1.0 - jnp.maximum(cn[p], 0.0) + jnp.minimum(cs[p], 0.0)
        own = own - jnp.maximum(ce[p], 0.0) + jnp.minimum(cw, 0.0)
        out.append((own, north, south, east, west))
    return out


def transport(x, coefs, is_top, is_bottom, both):
    above, below = shifted(x, ROWS - 1, is_top), shifted(x, 1, is_bottom)
    out = []
    for p in range(2 if both else 1):
        own, north, south, east, west = coefs[p]
        sides = east * pltpu.roll(x[p], LANES - 1, 1) + west * pltpu.roll(x[p], 1, 1)
        out.append((own * x[p] + sides) + (north * above[p] + south * below[p]))
    return tuple(out)


def remap(count, out_ref, first_tile, prefix, final, top, inverse, h, low, high, gap):
    inverse_h = 1.0 / h
    slot = iota(1) // SPARE
    zero = jnp.zeros((ROWS, LANES), jnp.float32)

    def targets(kb, last):
        base = 1.0 + h * (8 * kb + 1).astype(jnp.float32)
        start = [prefix[f, low(kb)] for f in range(count)]

        def layers(jq, acc):
            acc = list(acc)
            for i in range(4):
                j = 4 * jq + i
                inv = inverse[j]
                u = (base - top[j]) * inv
                stride = h * inv
                values = [final[f, j] for f in range(count)]
                for k in range(8):
                    w = jnp.minimum(jnp.maximum(u, 0.0), 1.0)
                    for f in range(count):
                        acc[count * k + f] = acc[count * k + f] + w * values[f]
                    if k < 7:
                        u = u + stride
            return tuple(acc)

        acc = lax.fori_loop(2 * low(kb), 2 * high(kb), layers, tuple(start) * 8)
        for half in range(2):
            for f in range(count):
                own = []
                for l in range(OWN):
                    k = OWN * half + l
                    below = acc[count * (k - 1) + f] if k else last[f]
                    own.append((acc[count * k + f] - below) * inverse_h)
                for i in range(3):
                    moved = turn(own[3], -SPARE * (1 + i))
                    out_ref[2 * kb + half, first_tile + 3 * f + i] = jnp.where(slot == gap, moved, own[i])
        return tuple(acc[7 * count :])

    lax.fori_loop(0, 8, targets, (zero,) * count)


def first_kernel(
    gap_ref, x_ref, c_ref, north_ref, south_ref,
    out_ref, push_ref, halo_c_ref, top, inverse, h_ref, bound_ref,
    halo_x, final, prefix, least, most,
):
    gap = gap_ref[0]
    is_top, is_bottom = iota(0) == ROWS - 1, iota(0) == 0
    join_strips(north_ref, south_ref, [halo_x.at[0], halo_x.at[1], halo_c_ref.at[0], halo_c_ref.at[1]])

    def group(g, carried):
        prefix[0, g] = carried[-1]
        least[g] = carried[-2]

        def layers(i, carried):
            runs = list(carried)
            for n in range(2):
                j = 8 * g + 2 * i + n
                mass = (x_ref[0, j], halo_x[0, j])
                theta = (x_ref[1, j], halo_x[1, j])
                coefs = coefficients((c_ref[0, j], halo_c_ref[0, j]), (c_ref[1, j], halo_c_ref[1, j]), is_top, is_bottom)
                for step in range(STEPS):
                    for p in range(2):
                        run = runs[2 * step + p]
                        middle = jnp.log(run + 0.5 * mass[p])
                        slope = pltpu.roll(middle, LANES - 1, 1) - pltpu.roll(middle, 1, 1)
                        push_ref[j, 2 * step + p] = 0.5 * theta[p] * slope
                        runs[2 * step + p] = run + mass[p]
                    both = step < STEPS - 1
                    mass = transport(mass, coefs, is_top, is_bottom, both)
                    theta = transport(theta, coefs, is_top, is_bottom, both)
                top[j] = runs[-2]
                inverse[j] = 1.0 / mass[0]
                final[0, j] = theta[0]
                runs[-2] = runs[-2] + mass[0]
                runs[-1] = runs[-1] + theta[0]
            return tuple(runs)

        return lax.fori_loop(0, 4, layers, carried)

    one, zero = jnp.ones((ROWS, LANES), jnp.float32), jnp.zeros((ROWS, LANES), jnp.float32)
    carried = lax.fori_loop(0, 8, group, (one,) * (2 * STEPS + 1) + (zero,))
    prefix[0, 8] = carried[-1]
    h = (carried[-2] - 1.0) * (1.0 / LEVELS)
    h_ref[...] = h

    inside = iota(1) // SPARE != gap
    inverse_h = 1.0 / h
    for b in range(1, 8):
        begin = (least[b] - 1.0) * inverse_h
        most[b] = jnp.max(jnp.where(inside, begin, 0.0))
        least_b = jnp.min(jnp.where(inside, begin, 1.0 * LEVELS))
        for kb in range(8):
            done = (most[b] <= 8.0 * kb + 0.99).astype(jnp.int32)
            begun = (least_b < 8.0 * kb + 8.01).astype(jnp.int32)
            bound_ref[kb] = done if b == 1 else bound_ref[kb] + done
            bound_ref[8 + kb] = 1 + begun if b == 1 else bound_ref[8 + kb] + begun

    remap(1, out_ref, 0, prefix, final, top, inverse, h, lambda kb: bound_ref[kb], lambda kb: bound_ref[8 + kb], gap)


def first_columns(gap, x, c, north, south):
    return pl.pallas_call(
        first_kernel,
        out_shape=(
            vmem(GROUP, 3),
            vmem(LEVELS, 2 * STEPS),
            vmem(2, LEVELS),
            vmem(LEVELS),
            vmem(LEVELS),
            vmem(),
            jax.ShapeDtypeStruct((16,), jnp.int32),
        ),
        in_specs=[IN_SMEM] + [IN_VMEM] * 4,
        out_specs=(IN_VMEM,) * 6 + (IN_SMEM,),
        scratch_shapes=[
            VMEM((2, LEVELS, ROWS, LANES), jnp.float32),
            VMEM((1, LEVELS, ROWS, LANES), jnp.float32),
            VMEM((1, 9, ROWS, LANES), jnp.float32),
            VMEM((8, ROWS, LANES), jnp.float32),
            SMEM((8,), jnp.float32),
        ],
        name="first_columns",
    )(gap, x, c, north, south)


def second_kernel(
    gap_ref, bound_ref, x_ref, c_ref, halo_c_ref, push_ref, north_ref, south_ref, top, inverse, h_ref, theta_ref,
    out_ref, halo, final, prefix,
):
    gap = gap_ref[0]
    is_top, is_bottom = iota(0) == ROWS - 1, iota(0) == 0
    join_strips(north_ref, south_ref, [halo.at[f] for f in range(3)])

    def group(g, carried):
        for f in range(3):
            prefix[f, g] = carried[f]

        def layers(i, carried):
            sums = list(carried)
            for n in range(2):
                j = 8 * g + 2 * i + n
                coefs = coefficients((c_ref[0, j], halo_c_ref[0, j]), (c_ref[1, j], halo_c_ref[1, j]), is_top, is_bottom)
                for f in range(3):
                    x = (x_ref[f, j], halo[f, j])
                    for step in range(STEPS):
                        if f == 0:
                            x = tuple(x[p] - push_ref[j, 2 * step + p] for p in range(2))
                        x = transport(x, coefs, is_top, is_bottom, step < STEPS - 1)
                    final[f, j] = x[0]
                    sums[f] = sums[f] + x[0]
            return tuple(sums)

        return lax.fori_loop(0, 4, layers, carried)

    zero = jnp.zeros((ROWS, LANES), jnp.float32)
    carried = lax.fori_loop(0, 8, group, (zero,) * 3)
    for f in range(3):
        prefix[f, 8] = carried[f]
    h = h_ref[...]
    remap(3, out_ref, 0, prefix, final, top, inverse, h, lambda kb: bound_ref[kb], lambda kb: bound_ref[8 + kb], gap)
    for d in range(GROUP):
        for i in range(3):
            out_ref[d, 9 + i] = theta_ref[d, i]
        out_ref[d, 12] = h


def second_columns(gap, bound, *arrays):
    return pl.pallas_call(
        second_kernel,
        out_shape=vmem(GROUP, 13),
        in_specs=[IN_SMEM] * 2 + [IN_VMEM] * len(arrays),
        out_specs=IN_VMEM,
        scratch_shapes=[
            VMEM((3, LEVELS, ROWS, LANES), jnp.float32),
            VMEM((3, LEVELS, ROWS, LANES), jnp.float32),
            VMEM((3, 9, ROWS, LANES), jnp.float32),
        ],
        name="second_columns",
    )(gap, bound, *arrays)


def unpack_kernel(x_ref, dp_ref, u_ref, v_ref, th_ref, tr_ref):
    lane = iota(1)
    slot = lane // SPARE

    def fourth(d, f):
        gap = (3 * d + 3) % 4
        t = [turn(x_ref[d, 3 * f + i], SPARE * (1 + i)) for i in range(3)]
        return jnp.where(slot == (gap + 1) % 4, t[0], jnp.where(slot == (gap + 2) % 4, t[1], t[2]))

    def merged(t, get):
        d = 4 * t // 3
        edge = (d + 1) * WIDTH - t * LANES
        return get(d) if edge >= LANES else jnp.where(lane < edge, get(d), get(d + 1))

    spans = [slice(t * LANES, (t + 1) * LANES) for t in range(TILES)]
    for t, span in enumerate(spans):
        h = merged(t, lambda d: x_ref[d, 12])
        for l in range(OWN):
            dp_ref[l, :, span] = h
    for f, ref in enumerate((u_ref, v_ref, tr_ref, th_ref)):
        last = [fourth(d, f) for d in range(GROUP)]
        for t, span in enumerate(spans):
            for l in range(3):
                ref[l, :, span] = merged(t, lambda d: x_ref[d, 3 * f + l])
            ref[3, :, span] = merged(t, lambda d: last[d])


def unpack(x):
    shape = jax.ShapeDtypeStruct((OWN, ROWS, TILES * LANES), jnp.float32)
    return pl.pallas_call(
        unpack_kernel,
        out_shape=(shape,) * 5,
        in_specs=[IN_VMEM],
        out_specs=(IN_VMEM,) * 5,
        name="unpack",
    )(x)


def body(*args):
    lats = lax.axis_size("lat")
    last = (lax.axis_index("lat") == lats - 1).astype(jnp.int32).reshape(1)
    gap = ((3 * lax.axis_index("lev") + 3) % 4).astype(jnp.int32).reshape(1)
    forward = [(i, i + 1) for i in range(lats - 1)]
    backward = [(b, a) for a, b in forward]

    def across(x):
        return lax.all_to_all(x, "lev", 0, 0, tiled=True)

    def strips(to_north, to_south):
        return lax.ppermute(to_south, "lat", backward), lax.ppermute(to_north, "lat", forward)

    sent_a, sent_b = pack(last, args)
    x_a, courant, to_north, to_south = edges(CHUNK_A, (2, 2), gap, across(sent_a))
    sent_b, to_north, to_south = lax.optimization_barrier((sent_b, to_north, to_south))
    north_a, south_a = strips(to_north, to_south)
    x_b, to_north, to_south = edges(CHUNK_B, (3,), gap, across(sent_b))
    north_b, south_b = strips(to_north, to_south)
    theta, push, halo_c, top, inverse, h, bound = first_columns(gap, x_a, courant, north_a, south_a)
    made = second_columns(gap, bound, x_b, courant, halo_c, push, north_b, south_b, top, inverse, h, theta)
    return tuple(unpack(across(made)))


def solution(mesh):
    spec = P("lev", "lat", None)
    return jax.shard_map(body, mesh=mesh, in_specs=(spec,) * 7, out_specs=(spec,) * 5, check_vma=False)
```

time: 291 us -> 140 us (0.48)
  local copies, waits for them, and re-layouts: 85.8 us -> 3.48 us
  blocking collectives: 96 us -> 27.7 us
  Pallas kernels: 0 us -> 40 us
  other arithmetic: 23 us -> 0 us
  waiting for transfers between devices: 42.2 us -> 30.8 us
  starting transfers between devices: 40.3 us -> 37 us
    all_gather x3 -> x0, blocking collectives: 58.8 us -> none  [entering(): gathered = lax.all_gather(part, axis)]
    unnamed x36 -> x12, local copies, waits for them, and re-layouts: 49 us -> 3.48 us
    pallas_call x0 -> x6, Pallas kernels: none -> 40 us  [the longest x1 13.7 us: second_columns(): pl.pallas_call(second_kernel, out_shape=vmem(GROUP, 13), in_specs=[IN_SME...]
    ppermute x7 -> x4, waiting for transfers between devices: 15.5 us -> 0.01 us  [the longest x2 0.01 us: strips(): lax.ppermute(to_north, 'lat', forward)]
    all_to_all x3 -> x0, local copies, waits for them, and re-layouts: 13.6 us -> none  [the longest x2 13.5 us: body(): lax.all_to_all(state, 'lev', split_axis=3, concat_axis=1, tiled=True)]
    sub x9 -> x0, local copies, waits for them, and re-layouts: 9.64 us -> none  [the longest x1 9.57 us: transport(): return centre - (north_flux - south_flux) - (east_flux - west_flux)]
    all_to_all x1, blocking collectives: 37.2 us -> 27.7 us  [across(): return lax.all_to_all(x, 'lev', 0, 0, tiled=True)]
    slice x36 -> x0, local copies, waits for them, and re-layouts: 6.33 us -> none  [the longest x8 1.99 us: push_winds(): jnp.roll(log_middle, 1, axis=-1)]
  transfers between devices with their start and end apart: 8 -> 6, of which waited for: 6 -> 2; matrix products, arithmetic and copies ran while one was open for 1% -> 0% of each run, Pallas kernels for 0% -> 12%
where the time goes in v2:
time: 140 us
  Pallas kernels  40 us (29%)
  starting transfers between devices  37 us (26%)
  waiting for transfers between devices  30.8 us (22%)
  blocking collectives  27.7 us (20%)
  local copies, waits for them, and re-layouts  3.48 us (2%)
    all_to_all x2, waiting for transfers between devices, across(): return lax.all_to_all(x, 'lev', 0, 0, tiled=True)  30.8 us
    all_to_all x1, blocking collectives, across(): return lax.all_to_all(x, 'lev', 0, 0, tiled=True)  27.7 us
    ppermute x2, starting transfers between devices, strips(): lax.ppermute(to_south, 'lat', backward)  21.9 us
    pallas_call x1, Pallas kernels, second_columns(): pl.pallas_call(second_kernel, out_shape=vmem(GROUP, 13), in_specs=[IN_SME...  13.7 us
    pallas_call x1, Pallas kernels, first_columns(): pl.pallas_call(first_kernel, out_shape=(vmem(GROUP, 3), vmem(LEVELS, 2 *...  13.3 us
    all_to_all x2, starting transfers between devices, across(): return lax.all_to_all(x, 'lev', 0, 0, tiled=True)  11.3 us
    pallas_call x2, Pallas kernels, edges(): pl.pallas_call(functools.partial(edges_kernel, chunk, outs), out_shape=tu...  6.92 us
    ppermute x2, starting transfers between devices, strips(): lax.ppermute(to_north, 'lat', forward)  3.84 us
  transfers between devices with their start and end apart: 6, of which 2 were waited for; matrix products, arithmetic and copies ran while one was open for 0% of the time, Pallas kernels for 12%

profile of v2, /device:TPU:7, one launch (start us, length us, event | category | flops | bytes accessed | tf_op | source)
XLA Modules:
  0.0 139.8 jit_solution(12869401759324247269)
XLA Ops:
  0.6 3.8 %pack.1 = (f32[16,13,8,128]{3,2,1,0:T(8,128)}, f32[16,10,8,128]{3,2,1,0:T(8,128)}) custom-call(s32[1]{0:T(128)} %bitcast.1.last_ref, f32[4,8,1536]{2,1,0:T(8,128)} %dp_ref.1, f32[4,8,1536]{2,1,0:T(8,128)} %u_ref.1, f32[4,8,1536]{2,1,0:T(8,128)} %v_ref.1, f32[4,8,1536]{2,1,0:T(8,128)} %th_ref.1, f32[4,8,1536]{2,1,0:T(8,128)} %tr_ref.1, f32[4,8,1536]{2,1,0:T(8,128)} %cn_ref.1, ...), custom_call_target="tpu_custom_call" | custom-call | tf_op jit(solution)/shard_map/pack/pallas_call | solution.py:96
  4.4 7.8 %all-to-all-start = ((f32[16,13,8,128]{3,2,1,0:T(8,128)}), f32[16,13,8,128]{3,2,1,0:T(8,128)S(1)}, u32[]{:S(2)}, u32[]{:S(2)}) async-start(f32[16,13,8,128]{3,2,1,0:T(8,128)} %get-tuple-element.24), calls=%async_computation | async-start | bytes 1703936 | tf_op jit(solution)/shard_map/all_to_all | solution.py:420
  12.2 24.0 %all-to-all-done.x_ref = f32[16,13,8,128]{3,2,1,0:T(8,128)S(1)} async-done(((f32[16,13,8,128]{3,2,1,0:T(8,128)}), f32[16,13,8,128]{3,2,1,0:T(8,128)S(1)}, u32[]{:S(2)}, u32[]{:S(2)}) %all-to-all-start) | async-done | bytes 852000 | tf_op jit(solution)/shard_map/all_to_all | solution.py:420
  36.2 0.0 copy-start
  36.2 0.9 copy-done
  37.2 3.6 %edges.2 = (f32[2,64,8,128]{3,2,1,0:T(8,128)}, f32[2,64,8,128]{3,2,1,0:T(8,128)}, f32[4,8,24,128]{3,2,1,0:T(8,128)}, f32[4,8,24,128]{3,2,1,0:T(8,128)}) custom-call(s32[1]{0:T(128)} %bitcast.gap_ref, f32[16,13,8,128]{3,2,1,0:T(8,128)} %copy-done), custom_call_target="tpu_custom_call" | custom-call | tf_op jit(solution)/shard_map/edges/pallas_call | solution.py:141
  40.8 3.5 %all-to-all-start.1 = ((f32[16,10,8,128]{3,2,1,0:T(8,128)}), f32[16,10,8,128]{3,2,1,0:T(8,128)S(1)}, u32[]{:S(2)}, u32[]{:S(2)}) async-start(f32[16,10,8,128]{3,2,1,0:T(8,128)} %get-tuple-element.33), calls=%async_computation.1 | async-start | bytes 1310720 | tf_op jit(solution)/shard_map/all_to_all | solution.py:420
  44.3 10.9 %collective-permute-start = (f32[4,8,24,128]{3,2,1,0:T(8,128)}, f32[4,8,24,128]{3,2,1,0:T(8,128)S(1)}, u32[]{:S(2)}, u32[]{:S(2)}) collective-permute-start(f32[4,8,24,128]{3,2,1,0:T(8,128)} %get-tuple-element.30), channel_id=1, source_target_pairs={{16,0},{32,16},{48,32},{64,48},{80,64},{96,80},{112,96},{128,112},... | collective-permute-start | bytes 1179656 | tf_op jit(solution)/shard_map/ppermute | solution.py:423
  55.2 1.9 %collective-permute-start.1 = (f32[4,8,24,128]{3,2,1,0:T(8,128)}, f32[4,8,24,128]{3,2,1,0:T(8,128)S(1)}, u32[]{:S(2)}, u32[]{:S(2)}) collective-permute-start(f32[4,8,24,128]{3,2,1,0:T(8,128)} %get-tuple-element.31), channel_id=1, source_target_pairs={{0,16},{16,32},{32,48},{48,64},{64,80},{80,96},{96,112},{112,128},... | collective-permute-start | bytes 1179656 | tf_op jit(solution)/shard_map/ppermute | solution.py:423
  57.2 6.8 %all-to-all-done.1.x_ref = f32[16,10,8,128]{3,2,1,0:T(8,128)S(1)} async-done(((f32[16,10,8,128]{3,2,1,0:T(8,128)}), f32[16,10,8,128]{3,2,1,0:T(8,128)S(1)}, u32[]{:S(2)}, u32[]{:S(2)}) %all-to-all-start.1) | async-done | bytes 655392 | tf_op jit(solution)/shard_map/all_to_all | solution.py:420
  64.0 0.0 copy-start.1
  64.0 0.8 copy-done.1
  64.8 3.3 %edges.3 = (f32[3,64,8,128]{3,2,1,0:T(8,128)}, f32[3,8,24,128]{3,2,1,0:T(8,128)}, f32[3,8,24,128]{3,2,1,0:T(8,128)}) custom-call(s32[1]{0:T(128)} %bitcast.gap_ref, f32[16,10,8,128]{3,2,1,0:T(8,128)} %copy-done.1), custom_call_target="tpu_custom_call" | custom-call | tf_op jit(solution)/shard_map/edges/pallas_call | solution.py:141
  68.1 10.9 %collective-permute-start.2 = (f32[3,8,24,128]{3,2,1,0:T(8,128)}, f32[3,8,24,128]{3,2,1,0:T(8,128)S(1)}, u32[]{:S(2)}, u32[]{:S(2)}) collective-permute-start(f32[3,8,24,128]{3,2,1,0:T(8,128)} %get-tuple-element.37), channel_id=1, source_target_pairs={{16,0},{32,16},{48,32},{64,48},{80,64},{96,80},{112,96},{128,112},... | collective-permute-start | bytes 884744 | tf_op jit(solution)/shard_map/ppermute | solution.py:423
  79.0 1.9 %collective-permute-start.3 = (f32[3,8,24,128]{3,2,1,0:T(8,128)}, f32[3,8,24,128]{3,2,1,0:T(8,128)S(1)}, u32[]{:S(2)}, u32[]{:S(2)}) collective-permute-start(f32[3,8,24,128]{3,2,1,0:T(8,128)} %get-tuple-element.38), channel_id=1, source_target_pairs={{0,16},{16,32},{32,48},{48,64},{64,80},{80,96},{96,112},{112,128},... | collective-permute-start | bytes 884744 | tf_op jit(solution)/shard_map/ppermute | solution.py:423
  80.9 0.0 collective-permute-done.north_ref
  81.0 0.0 copy-start.2
  81.0 0.0 collective-permute-done.1.south_ref
  81.0 0.0 copy-start.3
  81.0 0.7 copy-done.2
  81.7 0.2 copy-done.3
  81.9 13.3 %first_columns.1 = (f32[16,3,8,128]{3,2,1,0:T(8,128)}, f32[64,6,8,128]{3,2,1,0:T(8,128)}, f32[2,64,8,128]{3,2,1,0:T(8,128)}, f32[64,8,128]{2,1,0:T(8,128)}, f32[...) custom-call(s32[1]{0:T(128)} %bitcast.gap_ref, f32[2,64,8,128]{3,2,1,0:T(8,128)} %get-tuple-element.25.x_ref, ...), custom_call_target="tpu_custom_call" | custom-call | tf_op jit(solution)/shard_map/first_columns/pallas_call | solution.py:294
  95.2 0.0 collective-permute-done.2.north_ref
  95.2 0.0 copy-start.4
  95.2 0.0 collective-permute-done.3.south_ref
  95.2 0.0 copy-start.5
  95.2 0.7 copy-done.4
  95.9 0.1 copy-done.5
  96.0 13.7 %second_columns.1 = f32[16,13,8,128]{3,2,1,0:T(8,128)} custom-call(s32[1]{0:T(128)} %bitcast.gap_ref, s32[16]{0:T(128)} %get-tuple-element.32.bound_ref, f32[3,64,8,128]{3,2,1,0:T(8,128)} %get-tuple-element.34.x_ref, f32[2,64,8,128]{3,2,1,0:T(8,128)} %get-tuple-element.26.c_ref, f32[2,64,8,128]{3,2,1,0:T(8,128)} %get-tuple-element.35.halo_c_ref, ...), custom_call_target="tpu_custom_call" | custom-call | tf_op jit(solution)/shard_map/second_columns/pallas_call | solution.py:360
  109.8 27.7 %all_to_all.15.x_ref = f32[16,13,8,128]{3,2,1,0:T(8,128)} all-to-all(f32[16,13,8,128]{3,2,1,0:T(8,128)} %second_columns.1), channel_id=1, replica_groups=mesh['lat'=32,'lev'=16] {'lev'}, dimensions={0} | all-to-all | bytes 1703936 | tf_op jit(solution)/shard_map/all_to_all | solution.py:420
  137.5 2.3 %unpack.1 = (f32[4,8,1536]{2,1,0:T(8,128)}, f32[4,8,1536]{2,1,0:T(8,128)}, f32[4,8,1536]{2,1,0:T(8,128)}, f32[4,8,1536]{2,1,0:T(8,128)}, f32[4,8,1536]{2,1,0:T(8,128)}) custom-call(f32[16,13,8,128]{3,2,1,0:T(8,128)} %all_to_all.15.x_ref), custom_call_target="tpu_custom_call" | custom-call | tf_op jit(solution)/shard_map/unpack/pallas_call | solution.py:403
Async XLA Ops:
  4.4 31.8 %all-to-all-start = ((f32[16,13,8,128]{3,2,1,0:T(8,128)}), f32[16,13,8,128]{3,2,1,0:T(8,128)S(1)}, u32[]{:S(2)}, u32[]{:S(2)}) async-start(f32[16,13,8,128]{3,2,1,0:T(8,128)} %get-tuple-element.24), calls=%async_computation | async-start | bytes 1703936 | tf_op jit(solution)/shard_map/all_to_all | solution.py:420
  36.2 0.9 copy-start
  40.8 23.2 %all-to-all-start.1 = ((f32[16,10,8,128]{3,2,1,0:T(8,128)}), f32[16,10,8,128]{3,2,1,0:T(8,128)S(1)}, u32[]{:S(2)}, u32[]{:S(2)}) async-start(f32[16,10,8,128]{3,2,1,0:T(8,128)} %get-tuple-element.33), calls=%async_computation.1 | async-start | bytes 1310720 | tf_op jit(solution)/shard_map/all_to_all | solution.py:420
  44.3 36.7 %collective-permute-start = (f32[4,8,24,128]{3,2,1,0:T(8,128)}, f32[4,8,24,128]{3,2,1,0:T(8,128)S(1)}, u32[]{:S(2)}, u32[]{:S(2)}) collective-permute-start(f32[4,8,24,128]{3,2,1,0:T(8,128)} %get-tuple-element.30), channel_id=1, source_target_pairs={{16,0},{32,16},{48,32},{64,48},{80,64},{96,80},{112,96},{128,112},... | collective-permute-start | bytes 1179656 | tf_op jit(solution)/shard_map/ppermute | solution.py:423
  55.2 25.7 %collective-permute-start.1 = (f32[4,8,24,128]{3,2,1,0:T(8,128)}, f32[4,8,24,128]{3,2,1,0:T(8,128)S(1)}, u32[]{:S(2)}, u32[]{:S(2)}) collective-permute-start(f32[4,8,24,128]{3,2,1,0:T(8,128)} %get-tuple-element.31), channel_id=1, source_target_pairs={{0,16},{16,32},{32,48},{48,64},{64,80},{80,96},{96,112},{112,128},... | collective-permute-start | bytes 1179656 | tf_op jit(solution)/shard_map/ppermute | solution.py:423
  64.0 0.8 copy-start.1
  68.1 27.1 %collective-permute-start.2 = (f32[3,8,24,128]{3,2,1,0:T(8,128)}, f32[3,8,24,128]{3,2,1,0:T(8,128)S(1)}, u32[]{:S(2)}, u32[]{:S(2)}) collective-permute-start(f32[3,8,24,128]{3,2,1,0:T(8,128)} %get-tuple-element.37), channel_id=1, source_target_pairs={{16,0},{32,16},{48,32},{64,48},{80,64},{96,80},{112,96},{128,112},... | collective-permute-start | bytes 884744 | tf_op jit(solution)/shard_map/ppermute | solution.py:423
  79.0 16.2 %collective-permute-start.3 = (f32[3,8,24,128]{3,2,1,0:T(8,128)}, f32[3,8,24,128]{3,2,1,0:T(8,128)S(1)}, u32[]{:S(2)}, u32[]{:S(2)}) collective-permute-start(f32[3,8,24,128]{3,2,1,0:T(8,128)} %get-tuple-element.38), channel_id=1, source_target_pairs={{0,16},{16,32},{32,48},{48,64},{64,80},{80,96},{96,112},{112,128},... | collective-permute-start | bytes 884744 | tf_op jit(solution)/shard_map/ppermute | solution.py:423
  81.0 0.8 copy-start.2
  81.0 0.9 copy-start.3
  95.2 0.7 copy-start.4
  95.2 0.8 copy-start.5

commit v3 on v2

--- a/solution.py
+++ b/solution.py
@@ -47,59 +47,67 @@
 
 
 def vmem(*shape):
-    return jax.ShapeDtypeStruct(shape + (ROWS, LANES), jnp.float32)
+    return VMEM(shape + (ROWS, LANES), jnp.float32)
 
 
 IN_VMEM = pl.BlockSpec(memory_space=VMEM)
 IN_SMEM = pl.BlockSpec(memory_space=SMEM)
-
-
-def pack_kernel(last_ref, dp_ref, u_ref, v_ref, th_ref, tr_ref, cn_ref, ce_ref, a_ref, b_ref):
+GRANT = pltpu.CompilerParams(vmem_limit_bytes=16 << 20)
+
+
+def near(*arrays):
+    return tuple(pltpu.with_memory_space_constraint(x, VMEM) for x in arrays)
+
+
+def pack_kernel(chunk, scaled, last_ref, *refs):
     lane = iota(1)
-    closed = jnp.logical_and(last_ref[0] > 0, iota(0) == ROWS - 1)
-
-    def load(ref, l, t):
-        x = ref[l, :, t * LANES : (t + 1) * LANES]
-        if any(ref is other for other in (u_ref, v_ref, th_ref, tr_ref)):
-            x = x * dp_ref[l, :, t * LANES : (t + 1) * LANES]
-        if ref is cn_ref:
+    slot = lane // SPARE
+    refs, out_ref = refs[:-1], refs[-1]
+    thickness = refs[0]
+    if scaled == "all":
+        refs = refs[1:]
+
+    def load(f, l, t):
+        span = slice(t * LANES, (t + 1) * LANES)
+        x = refs[f][l, :, span]
+        if scaled == "all" or f == 1:
+            x = x * thickness[l, :, span]
+        elif f == 2:
+            closed = jnp.logical_and(last_ref[0] > 0, iota(0) == ROWS - 1)
             x = jnp.where(closed, 0.0, x)
         return x
 
-    for chunk, refs, out_ref in (
-        (CHUNK_A, (dp_ref, th_ref, cn_ref, ce_ref), a_ref),
-        (CHUNK_B, (u_ref, v_ref, tr_ref), b_ref),
-    ):
-        where = places(chunk)
-        for d in range(GROUP):
-            gap = (3 * d + 3) % 4
-            first = d * WIDTH - 16
-            a, off = (first // LANES) % TILES, first % LANES
-            slot = lane // SPARE
-            rel = (lane - gap * SPARE) % LANES
-            sides = jnp.zeros((ROWS, LANES), jnp.float32)
-            for f, ref in enumerate(refs):
-                east, west = chunk[f]
-                own = []
-                for l in range(OWN):
-                    x = jnp.where(lane >= off, load(ref, l, a), load(ref, l, (a + 1) % TILES))
-                    at_east, at_west = where[f][l]
-                    sides = jnp.where(rel >= at_east, turn(x, at_east), sides)
-                    sides = jnp.where(rel >= at_west, turn(x, at_west - (SPARE - west)), sides)
-                    own.append(x)
-                for i in range(3):
-                    out_ref[d, 3 * f + i] = jnp.where(slot == gap, turn(own[3], -SPARE * (1 + i)), own[i])
-            out_ref[d, 3 * len(chunk)] = sides
-
-
-def pack(last, args):
+    where = places(chunk)
+    for d in range(GROUP):
+        gap = (3 * d + 3) % 4
+        first = d * WIDTH - 16
+        a, off = (first // LANES) % TILES, first % LANES
+        rel = (lane - gap * SPARE) % LANES
+        sides = jnp.zeros((ROWS, LANES), jnp.float32)
+        for f in range(len(chunk)):
+            east, west = chunk[f]
+            own = []
+            for l in range(OWN):
+                x = jnp.where(lane >= off, load(f, l, a), load(f, l, (a + 1) % TILES))
+                at_east, at_west = where[f][l]
+                sides = jnp.where(rel >= at_east, turn(x, at_east), sides)
+                sides = jnp.where(rel >= at_west, turn(x, at_west - (SPARE - west)), sides)
+                own.append(x)
+            for i in range(3):
+                out_ref[d, 3 * f + i] = jnp.where(slot == gap, turn(own[3], -SPARE * (1 + i)), own[i])
+        out_ref[d, 3 * len(chunk)] = sides
+
+
+def pack(chunk, scaled, last, args):
     return pl.pallas_call(
-        pack_kernel,
-        out_shape=(vmem(GROUP, tile_count(CHUNK_A)), vmem(GROUP, tile_count(CHUNK_B))),
-        in_specs=[IN_SMEM] + [IN_VMEM] * 7,
-        out_specs=(IN_VMEM,) * 2,
-        name="pack",
-    )(last, *args)
+        functools.partial(pack_kernel, chunk, scaled),
+        out_shape=vmem(GROUP, tile_count(chunk)),
+        in_specs=[IN_SMEM] + [IN_VMEM] * len(args),
+        out_specs=IN_VMEM,
+        compiler_params=GRANT,
+        cost_estimate=pl.CostEstimate(flops=10**6, bytes_accessed=4 << 20, transcendentals=0),
+        name="pack_" + scaled,
+    )(last, *(pltpu.with_memory_space_constraint(x, pltpu.HBM) for x in args))
 
 
 def edges_kernel(chunk, outs, gap_ref, x_ref, *refs):
@@ -137,14 +145,15 @@
 
 
 def edges(chunk, outs, gap, x):
-    strip = jax.ShapeDtypeStruct((len(chunk), 8, 24, LANES), jnp.float32)
+    strip = VMEM((len(chunk), 8, 24, LANES), jnp.float32)
     return pl.pallas_call(
         functools.partial(edges_kernel, chunk, outs),
         out_shape=tuple(vmem(n, LEVELS) for n in outs) + (strip, strip),
         in_specs=[IN_SMEM, IN_VMEM],
         out_specs=(IN_VMEM,) * (len(outs) + 2),
+        compiler_params=GRANT,
         name="edges",
-    )(gap, x)
+    )(gap, *near(x))
 
 
 def join_strips(north_ref, south_ref, halo_refs):
@@ -200,8 +209,8 @@
 
         def layers(jq, acc):
             acc = list(acc)
-            for i in range(4):
-                j = 4 * jq + i
+            for i in range(8):
+                j = 8 * jq + i
                 inv = inverse[j]
                 u = (base - top[j]) * inv
                 stride = h * inv
@@ -214,7 +223,7 @@
                         u = u + stride
             return tuple(acc)
 
-        acc = lax.fori_loop(2 * low(kb), 2 * high(kb), layers, tuple(start) * 8)
+        acc = lax.fori_loop(low(kb), high(kb), layers, tuple(start) * 8)
         for half in range(2):
             for f in range(count):
                 own = []
@@ -245,8 +254,8 @@
 
         def layers(i, carried):
             runs = list(carried)
-            for n in range(2):
-                j = 8 * g + 2 * i + n
+            for n in range(4):
+                j = 8 * g + 4 * i + n
                 mass = (x_ref[0, j], halo_x[0, j])
                 theta = (x_ref[1, j], halo_x[1, j])
                 coefs = coefficients((c_ref[0, j], halo_c_ref[0, j]), (c_ref[1, j], halo_c_ref[1, j]), is_top, is_bottom)
@@ -267,7 +276,7 @@
                 runs[-1] = runs[-1] + theta[0]
             return tuple(runs)
 
-        return lax.fori_loop(0, 4, layers, carried)
+        return lax.fori_loop(0, 2, layers, carried)
 
     one, zero = jnp.ones((ROWS, LANES), jnp.float32), jnp.zeros((ROWS, LANES), jnp.float32)
     carried = lax.fori_loop(0, 8, group, (one,) * (2 * STEPS + 1) + (zero,))
@@ -311,8 +320,9 @@
             VMEM((8, ROWS, LANES), jnp.float32),
             SMEM((8,), jnp.float32),
         ],
+        compiler_params=GRANT,
         name="first_columns",
-    )(gap, x, c, north, south)
+    )(gap, *near(x, c, north, south))
 
 
 def second_kernel(
@@ -329,8 +339,8 @@
 
         def layers(i, carried):
             sums = list(carried)
-            for n in range(2):
-                j = 8 * g + 2 * i + n
+            for n in range(4):
+                j = 8 * g + 4 * i + n
                 coefs = coefficients((c_ref[0, j], halo_c_ref[0, j]), (c_ref[1, j], halo_c_ref[1, j]), is_top, is_bottom)
                 for f in range(3):
                     x = (x_ref[f, j], halo[f, j])
@@ -342,7 +352,7 @@
                     sums[f] = sums[f] + x[0]
             return tuple(sums)
 
-        return lax.fori_loop(0, 4, layers, carried)
+        return lax.fori_loop(0, 2, layers, carried)
 
     zero = jnp.zeros((ROWS, LANES), jnp.float32)
     carried = lax.fori_loop(0, 8, group, (zero,) * 3)
@@ -367,8 +377,9 @@
             VMEM((3, LEVELS, ROWS, LANES), jnp.float32),
             VMEM((3, 9, ROWS, LANES), jnp.float32),
         ],
+        compiler_params=GRANT,
         name="second_columns",
-    )(gap, bound, *arrays)
+    )(gap, bound, *near(*arrays))
 
 
 def unpack_kernel(x_ref, dp_ref, u_ref, v_ref, th_ref, tr_ref):
@@ -405,15 +416,16 @@
         out_shape=(shape,) * 5,
         in_specs=[IN_VMEM],
         out_specs=(IN_VMEM,) * 5,
+        compiler_params=GRANT,
         name="unpack",
-    )(x)
-
-
-def body(*args):
+    )(*near(x))
+
+
+def body(dp, u, v, th, tr, cn, ce):
     lats = lax.axis_size("lat")
     last = (lax.axis_index("lat") == lats - 1).astype(jnp.int32).reshape(1)
     gap = ((3 * lax.axis_index("lev") + 3) % 4).astype(jnp.int32).reshape(1)
-    forward = [(i, i + 1) for i in range(lats - 1)]
+    forward = [(i, (i + 1) % lats) for i in range(lats)]
     backward = [(b, a) for a, b in forward]
 
     def across(x):
@@ -422,9 +434,10 @@
     def strips(to_north, to_south):
         return lax.ppermute(to_south, "lat", backward), lax.ppermute(to_north, "lat", forward)
 
-    sent_a, sent_b = pack(last, args)
-    x_a, courant, to_north, to_south = edges(CHUNK_A, (2, 2), gap, across(sent_a))
-    sent_b, to_north, to_south = lax.optimization_barrier((sent_b, to_north, to_south))
+    held_a = across(pack(CHUNK_A, "one", last, (dp, th, cn, ce)))
+    sent_b = pack(CHUNK_B, "all", last, (dp, u, v, tr))
+    x_a, courant, to_north, to_south = edges(CHUNK_A, (2, 2), gap, held_a)
+
     north_a, south_a = strips(to_north, to_south)
     x_b, to_north, to_south = edges(CHUNK_B, (3,), gap, across(sent_b))
     north_b, south_b = strips(to_north, to_south)

time: 140 us -> 124 us (0.89)
  the two profiles are of different devices: /device:TPU:7 before, /device:TPU:1 now
where the time goes in v3:
time: 124 us
  starting transfers between devices  39.9 us (32%)
  waiting for transfers between devices  30.9 us (25%)
  blocking collectives  28.1 us (23%)
  Pallas kernels  24.3 us (20%)
    all_to_all x1, blocking collectives, across(): return lax.all_to_all(x, 'lev', 0, 0, tiled=True)  28.1 us
    all_to_all x2, waiting for transfers between devices, across(): return lax.all_to_all(x, 'lev', 0, 0, tiled=True)  26.7 us
    ppermute x2, starting transfers between devices, strips(): lax.ppermute(to_south, 'lat', backward)  22.3 us
    all_to_all x2, starting transfers between devices, across(): return lax.all_to_all(x, 'lev', 0, 0, tiled=True)  13.7 us
    pallas_call x1, Pallas kernels, second_columns(): pl.pallas_call(second_kernel, out_shape=vmem(GROUP, 13), in_specs=[IN_SME...  8.09 us
    pallas_call x1, Pallas kernels, first_columns(): pl.pallas_call(first_kernel, out_shape=(vmem(GROUP, 3), vmem(LEVELS, 2 *...  7.1 us
    pallas_call x2, Pallas kernels, pack(): pl.pallas_call(functools.partial(pack_kernel, chunk, scaled), out_shape=v...  5.6 us
    ppermute x2, waiting for transfers between devices, strips(): lax.ppermute(to_north, 'lat', forward)  4.14 us
  transfers between devices with their start and end apart: 6, of which 3 were waited for; matrix products, arithmetic and copies ran while one was open for 0% of the time, Pallas kernels for 10%

profile of v3, /device:TPU:1, one launch (start us, length us, event | category | flops | bytes accessed | tf_op | source)
XLA Modules:
  0.0 123.9 jit_solution(11308313978019831724)
XLA Ops:
  0.6 2.9 %pack_one.1 = f32[16,13,8,128]{3,2,1,0:T(8,128)} custom-call(s32[1]{0:T(128)} %bitcast.1.last_ref, f32[4,8,1536]{2,1,0:T(8,128)} %refs_0_.3, f32[4,8,1536]{2,1,0:T(8,128)} %refs_1_.2, f32[4,8,1536]{2,1,0:T(8,128)} %refs_2_.2, f32[4,8,1536]{2,1,0:T(8,128)} %refs_3_.2), custom_call_target="tpu_custom_call" | custom-call | flops 1000000 | bytes 4194304 | tf_op jit(solution)/shard_map/pack_one/pallas_call | solution.py:102
  3.6 10.2 %all-to-all-start = ((f32[16,13,8,128]{3,2,1,0:T(8,128)}), f32[16,13,8,128]{3,2,1,0:T(8,128)S(1)}, u32[]{:S(2)}, u32[]{:S(2)}) async-start(f32[16,13,8,128]{3,2,1,0:T(8,128)} %pack_one.1), calls=%async_computation | async-start | bytes 1703936 | tf_op jit(solution)/shard_map/all_to_all | solution.py:432
  13.8 2.7 %pack_all.1 = f32[16,10,8,128]{3,2,1,0:T(8,128)} custom-call(s32[1]{0:T(128)} %bitcast.1.last_ref, f32[4,8,1536]{2,1,0:T(8,128)} %refs_0_.3, f32[4,8,1536]{2,1,0:T(8,128)} %refs_1_.3, f32[4,8,1536]{2,1,0:T(8,128)} %refs_2_.3, f32[4,8,1536]{2,1,0:T(8,128)} %refs_3_.3), custom_call_target="tpu_custom_call" | custom-call | flops 1000000 | bytes 4194304 | tf_op jit(solution)/shard_map/pack_all/pallas_call | solution.py:102
  16.5 21.4 %all-to-all-done.x_ref = f32[16,13,8,128]{3,2,1,0:T(8,128)S(1)} async-done(((f32[16,13,8,128]{3,2,1,0:T(8,128)}), f32[16,13,8,128]{3,2,1,0:T(8,128)S(1)}, u32[]{:S(2)}, u32[]{:S(2)}) %all-to-all-start) | async-done | bytes 852000 | tf_op jit(solution)/shard_map/all_to_all | solution.py:432
  37.9 3.5 %all-to-all-start.1 = ((f32[16,10,8,128]{3,2,1,0:T(8,128)}), f32[16,10,8,128]{3,2,1,0:T(8,128)S(1)}, u32[]{:S(2)}, u32[]{:S(2)}) async-start(f32[16,10,8,128]{3,2,1,0:T(8,128)} %pack_all.1), calls=%async_computation.1 | async-start | bytes 1310720 | tf_op jit(solution)/shard_map/all_to_all | solution.py:432
  41.4 1.2 %edges.2 = (f32[2,64,8,128]{3,2,1,0:T(8,128)S(1)}, f32[2,64,8,128]{3,2,1,0:T(8,128)S(1)}, f32[4,8,24,128]{3,2,1,0:T(8,128)S(1)}, f32[4,8,24,128]{3,2,1,0:T(8,128)S(1)}) custom-call(s32[1]{0:T(128)} %bitcast.gap_ref, f32[16,13,8,128]{3,2,1,0:T(8,128)S(1)} %all-to-all-done.x_ref), custom_call_target="tpu_custom_call" | custom-call | tf_op jit(solution)/shard_map/edges/pallas_call | solution.py:149
  42.7 11.2 %collective-permute-start = (f32[4,8,24,128]{3,2,1,0:T(8,128)S(1)}, f32[4,8,24,128]{3,2,1,0:T(8,128)S(1)}, u32[]{:S(2)}, u32[]{:S(2)}) collective-permute-start(f32[4,8,24,128]{3,2,1,0:T(8,128)S(1)} %get-tuple-element.21), channel_id=1, source_target_pairs={{16,0},{32,16},{48,32},{64,48},{80,64},{96,80},{112,96},{128,112},... | collective-permute-start | bytes 1179656 | tf_op jit(solution)/shard_map/ppermute | solution.py:435
  53.9 1.9 %collective-permute-start.1 = (f32[4,8,24,128]{3,2,1,0:T(8,128)S(1)}, f32[4,8,24,128]{3,2,1,0:T(8,128)S(1)}, u32[]{:S(2)}, u32[]{:S(2)}) collective-permute-start(f32[4,8,24,128]{3,2,1,0:T(8,128)S(1)} %get-tuple-element.22), channel_id=1, source_target_pairs={{0,16},{16,32},{32,48},{48,64},{64,80},{80,96},{96,112},{112,128},... | collective-permute-start | bytes 1179656 | tf_op jit(solution)/shard_map/ppermute | solution.py:435
  55.8 5.3 %all-to-all-done.1.x_ref = f32[16,10,8,128]{3,2,1,0:T(8,128)S(1)} async-done(((f32[16,10,8,128]{3,2,1,0:T(8,128)}), f32[16,10,8,128]{3,2,1,0:T(8,128)S(1)}, u32[]{:S(2)}, u32[]{:S(2)}) %all-to-all-start.1) | async-done | bytes 655392 | tf_op jit(solution)/shard_map/all_to_all | solution.py:432
  61.1 1.1 edges.3
  62.2 11.2 %collective-permute-start.2 = (f32[3,8,24,128]{3,2,1,0:T(8,128)S(1)}, f32[3,8,24,128]{3,2,1,0:T(8,128)S(1)}, u32[]{:S(2)}, u32[]{:S(2)}) collective-permute-start(f32[3,8,24,128]{3,2,1,0:T(8,128)S(1)} %get-tuple-element.27), channel_id=1, source_target_pairs={{16,0},{32,16},{48,32},{64,48},{80,64},{96,80},{112,96},{128,112},... | collective-permute-start | bytes 884744 | tf_op jit(solution)/shard_map/ppermute | solution.py:435
  73.4 1.9 %collective-permute-start.3 = (f32[3,8,24,128]{3,2,1,0:T(8,128)S(1)}, f32[3,8,24,128]{3,2,1,0:T(8,128)S(1)}, u32[]{:S(2)}, u32[]{:S(2)}) collective-permute-start(f32[3,8,24,128]{3,2,1,0:T(8,128)S(1)} %get-tuple-element.28), channel_id=1, source_target_pairs={{0,16},{16,32},{32,48},{48,64},{64,80},{80,96},{96,112},{112,128},... | collective-permute-start | bytes 884744 | tf_op jit(solution)/shard_map/ppermute | solution.py:435
  75.3 0.0 collective-permute-done.north_ref
  75.3 0.0 collective-permute-done.1.south_ref
  75.3 7.1 %first_columns.1 = (f32[16,3,8,128]{3,2,1,0:T(8,128)S(1)}, f32[64,6,8,128]{3,2,1,0:T(8,128)S(1)}, f32[2,64,8,128]{3,2,1,0:T(8,128)S(1)}, f32[64,8,128]{2,1,0:T(8...) custom-call(s32[1]{0:T(128)} %bitcast.gap_ref, ...), custom_call_target="tpu_custom_call" | custom-call | tf_op jit(solution)/shard_map/first_columns/pallas_call | solution.py:303
  82.4 0.0 collective-permute-done.2.north_ref
  82.4 4.1 %collective-permute-done.3.south_ref = f32[3,8,24,128]{3,2,1,0:T(8,128)S(1)} collective-permute-done((f32[3,8,24,128]{3,2,1,0:T(8,128)S(1)}, f32[3,8,24,128]{3,2,1,0:T(8,128)S(1)}, u32[]{:S(2)}, u32[]{:S(2)}) %collective-permute-start.3) | collective-permute-done | bytes 294944 | tf_op jit(solution)/shard_map/ppermute | solution.py:435
  86.6 8.1 %second_columns.1 = f32[16,13,8,128]{3,2,1,0:T(8,128)S(1)} custom-call(s32[1]{0:T(128)} %bitcast.gap_ref, s32[16]{0:T(128)S(1)} %get-tuple-element.23.bound_ref, f32[3,64,8,128]{3,2,1,0:T(8,128)S(1)} %get-tuple-element.24.x_ref, f32[2,64,8,128]{3,2,1,0:T(8,128)S(1)} %get-tuple-element.20.c_ref, f32[2,64,8,128]{3,2,1,0:T(8,128)S(1)} %get-tuple-element.25.halo_c_ref, ...), custom_call_target="tpu_custom_call" | custom-call | tf_op jit(solution)/shard_map/second_columns/pallas_call | solution.py:370
  94.7 28.1 %all_to_all.15.x_ref = f32[16,13,8,128]{3,2,1,0:T(8,128)S(1)} all-to-all(f32[16,13,8,128]{3,2,1,0:T(8,128)S(1)} %second_columns.1), channel_id=1, replica_groups=mesh['lat'=32,'lev'=16] {'lev'}, dimensions={0} | all-to-all | bytes 1703936 | tf_op jit(solution)/shard_map/all_to_all | solution.py:432
  122.8 1.1 unpack.1
Async XLA Ops:
  3.6 34.3 %all-to-all-start = ((f32[16,13,8,128]{3,2,1,0:T(8,128)}), f32[16,13,8,128]{3,2,1,0:T(8,128)S(1)}, u32[]{:S(2)}, u32[]{:S(2)}) async-start(f32[16,13,8,128]{3,2,1,0:T(8,128)} %pack_one.1), calls=%async_computation | async-start | bytes 1703936 | tf_op jit(solution)/shard_map/all_to_all | solution.py:432
  37.9 23.2 %all-to-all-start.1 = ((f32[16,10,8,128]{3,2,1,0:T(8,128)}), f32[16,10,8,128]{3,2,1,0:T(8,128)S(1)}, u32[]{:S(2)}, u32[]{:S(2)}) async-start(f32[16,10,8,128]{3,2,1,0:T(8,128)} %pack_all.1), calls=%async_computation.1 | async-start | bytes 1310720 | tf_op jit(solution)/shard_map/all_to_all | solution.py:432
  42.7 32.6 %collective-permute-start = (f32[4,8,24,128]{3,2,1,0:T(8,128)S(1)}, f32[4,8,24,128]{3,2,1,0:T(8,128)S(1)}, u32[]{:S(2)}, u32[]{:S(2)}) collective-permute-start(f32[4,8,24,128]{3,2,1,0:T(8,128)S(1)} %get-tuple-element.21), channel_id=1, source_target_pairs={{16,0},{32,16},{48,32},{64,48},{80,64},{96,80},{112,96},{128,112},... | collective-permute-start | bytes 1179656 | tf_op jit(solution)/shard_map/ppermute | solution.py:435
  53.9 21.5 %collective-permute-start.1 = (f32[4,8,24,128]{3,2,1,0:T(8,128)S(1)}, f32[4,8,24,128]{3,2,1,0:T(8,128)S(1)}, u32[]{:S(2)}, u32[]{:S(2)}) collective-permute-start(f32[4,8,24,128]{3,2,1,0:T(8,128)S(1)} %get-tuple-element.22), channel_id=1, source_target_pairs={{0,16},{16,32},{32,48},{48,64},{64,80},{80,96},{96,112},{112,128},... | collective-permute-start | bytes 1179656 | tf_op jit(solution)/shard_map/ppermute | solution.py:435
  62.2 20.2 %collective-permute-start.2 = (f32[3,8,24,128]{3,2,1,0:T(8,128)S(1)}, f32[3,8,24,128]{3,2,1,0:T(8,128)S(1)}, u32[]{:S(2)}, u32[]{:S(2)}) collective-permute-start(f32[3,8,24,128]{3,2,1,0:T(8,128)S(1)} %get-tuple-element.27), channel_id=1, source_target_pairs={{16,0},{32,16},{48,32},{64,48},{80,64},{96,80},{112,96},{128,112},... | collective-permute-start | bytes 884744 | tf_op jit(solution)/shard_map/ppermute | solution.py:435
  73.4 13.2 %collective-permute-start.3 = (f32[3,8,24,128]{3,2,1,0:T(8,128)S(1)}, f32[3,8,24,128]{3,2,1,0:T(8,128)S(1)}, u32[]{:S(2)}, u32[]{:S(2)}) collective-permute-start(f32[3,8,24,128]{3,2,1,0:T(8,128)S(1)} %get-tuple-element.28), channel_id=1, source_target_pairs={{0,16},{16,32},{32,48},{48,64},{64,80},{80,96},{96,112},{112,128},... | collective-permute-start | bytes 884744 | tf_op jit(solution)/shard_map/ppermute | solution.py:435

commit v4 on v3

--- a/solution.py
+++ b/solution.py
@@ -111,7 +111,8 @@
 
 
 def edges_kernel(chunk, outs, gap_ref, x_ref, *refs):
-    north_ref, south_ref = refs[-2:]
+    first_ref, second_ref = refs[-2:]
+    even = gap_ref[1] > 0
     out_refs = [ref.at[k] for ref, n in zip(refs[:-2], outs) for k in range(n)]
     where = places(chunk)
     gap = gap_ref[0]
@@ -137,8 +138,9 @@
                     x = jnp.where(in_west, turn(sides, SPARE - west - at_west), x)
                     i = OWN * half + l
                     out_refs[f][OWN * src + l] = x
-                    north_ref[f, g, 3 * i : 3 * i + 3, :] = x[5:8]
-                    south_ref[f, g, 3 * i : 3 * i + 3, :] = x[0:3]
+                    north = pltpu.roll(x, 3, 0)
+                    first_ref[f, g, 3 * i : 3 * i + 3, :] = jnp.where(even, north, x)[0:3]
+                    second_ref[f, g, 3 * i : 3 * i + 3, :] = jnp.where(even, x, north)[0:3]
         return 0
 
     lax.fori_loop(0, 8, group, 0)
@@ -156,15 +158,16 @@
     )(gap, *near(x))
 
 
-def join_strips(north_ref, south_ref, halo_refs):
+def join_strips(even, first_ref, second_ref, halo_refs):
     for f, halo in enumerate(halo_refs):
         halo[...] = jnp.zeros(halo.shape, jnp.float32)
 
     def group(g, _):
         for f, halo in enumerate(halo_refs):
             for i in range(8):
-                halo[8 * g + i, 0:3, :] = north_ref[f, g, 3 * i : 3 * i + 3, :]
-                halo[8 * g + i, 5:8, :] = south_ref[f, g, 3 * i : 3 * i + 3, :]
+                a, b = (ref[f, g, 3 * i : 3 * i + 3, :] for ref in (first_ref, second_ref))
+                halo[8 * g + i, 0:3, :] = jnp.where(even, a, b)
+                halo[8 * g + i, 5:8, :] = jnp.where(even, b, a)
         return 0
 
     lax.fori_loop(0, 8, group, 0)
@@ -240,13 +243,13 @@
 
 
 def first_kernel(
-    gap_ref, x_ref, c_ref, north_ref, south_ref,
+    gap_ref, x_ref, c_ref, first_ref, second_ref,
     out_ref, push_ref, halo_c_ref, top, inverse, h_ref, bound_ref,
     halo_x, final, prefix, least, most,
 ):
     gap = gap_ref[0]
     is_top, is_bottom = iota(0) == ROWS - 1, iota(0) == 0
-    join_strips(north_ref, south_ref, [halo_x.at[0], halo_x.at[1], halo_c_ref.at[0], halo_c_ref.at[1]])
+    join_strips(gap_ref[1] > 0, first_ref, second_ref, [halo_x.at[0], halo_x.at[1], halo_c_ref.at[0], halo_c_ref.at[1]])
 
     def group(g, carried):
         prefix[0, g] = carried[-1]
@@ -326,12 +329,12 @@
 
 
 def second_kernel(
-    gap_ref, bound_ref, x_ref, c_ref, halo_c_ref, push_ref, north_ref, south_ref, top, inverse, h_ref, theta_ref,
+    gap_ref, bound_ref, x_ref, c_ref, halo_c_ref, push_ref, first_ref, second_ref, top, inverse, h_ref, theta_ref,
     out_ref, halo, final, prefix,
 ):
     gap = gap_ref[0]
     is_top, is_bottom = iota(0) == ROWS - 1, iota(0) == 0
-    join_strips(north_ref, south_ref, [halo.at[f] for f in range(3)])
+    join_strips(gap_ref[1] > 0, first_ref, second_ref, [halo.at[f] for f in range(3)])
 
     def group(g, carried):
         for f in range(3):
@@ -424,25 +427,25 @@
 def body(dp, u, v, th, tr, cn, ce):
     lats = lax.axis_size("lat")
     last = (lax.axis_index("lat") == lats - 1).astype(jnp.int32).reshape(1)
-    gap = ((3 * lax.axis_index("lev") + 3) % 4).astype(jnp.int32).reshape(1)
-    forward = [(i, (i + 1) % lats) for i in range(lats)]
-    backward = [(b, a) for a, b in forward]
+    gap = jnp.stack([(3 * lax.axis_index("lev") + 3) % 4, 1 - lax.axis_index("lat") % 2]).astype(jnp.int32)
+    swaps = [[(i, i + 1) for i in range(start, lats - 1, 2)] for start in (0, 1)]
+    swaps = [pairs + [(b, a) for a, b in pairs] for pairs in swaps]
 
     def across(x):
         return lax.all_to_all(x, "lev", 0, 0, tiled=True)
 
-    def strips(to_north, to_south):
-        return lax.ppermute(to_south, "lat", backward), lax.ppermute(to_north, "lat", forward)
+    def strips(first, second):
+        return lax.ppermute(first, "lat", swaps[0]), lax.ppermute(second, "lat", swaps[1])
 
     held_a = across(pack(CHUNK_A, "one", last, (dp, th, cn, ce)))
     sent_b = pack(CHUNK_B, "all", last, (dp, u, v, tr))
-    x_a, courant, to_north, to_south = edges(CHUNK_A, (2, 2), gap, held_a)
-
-    north_a, south_a = strips(to_north, to_south)
-    x_b, to_north, to_south = edges(CHUNK_B, (3,), gap, across(sent_b))
-    north_b, south_b = strips(to_north, to_south)
-    theta, push, halo_c, top, inverse, h, bound = first_columns(gap, x_a, courant, north_a, south_a)
-    made = second_columns(gap, bound, x_b, courant, halo_c, push, north_b, south_b, top, inverse, h, theta)
+    x_a, courant, first, second = edges(CHUNK_A, (2, 2), gap, held_a)
+
+    first_a, second_a = strips(first, second)
+    x_b, first, second = edges(CHUNK_B, (3,), gap, across(sent_b))
+    first_b, second_b = strips(first, second)
+    theta, push, halo_c, top, inverse, h, bound = first_columns(gap, x_a, courant, first_a, second_a)
+    made = second_columns(gap, bound, x_b, courant, halo_c, push, first_b, second_b, top, inverse, h, theta)
     return tuple(unpack(across(made)))
 
 

time: 124 us -> 118 us (0.952)
  the two profiles are of different devices: /device:TPU:1 before, /device:TPU:7 now
where the time goes in v4:
time: 118 us
  starting transfers between devices  37.5 us (32%)
  blocking collectives  27.6 us (23%)
  waiting for transfers between devices  26 us (22%)
  Pallas kernels  25.9 us (22%)
    all_to_all x1, blocking collectives, across(): return lax.all_to_all(x, 'lev', 0, 0, tiled=True)  27.6 us
    all_to_all x2, waiting for transfers between devices, across(): return lax.all_to_all(x, 'lev', 0, 0, tiled=True)  26 us
    ppermute x2, starting transfers between devices, strips(): lax.ppermute(second, 'lat', swaps[1])  18.2 us
    all_to_all x2, starting transfers between devices, across(): return lax.all_to_all(x, 'lev', 0, 0, tiled=True)  11.3 us
    pallas_call x1, Pallas kernels, second_columns(): pl.pallas_call(second_kernel, out_shape=vmem(GROUP, 13), in_specs=[IN_SME...  8.1 us
    ppermute x2, starting transfers between devices, strips(): lax.ppermute(first, 'lat', swaps[0])  8 us
    pallas_call x1, Pallas kernels, first_columns(): pl.pallas_call(first_kernel, out_shape=(vmem(GROUP, 3), vmem(LEVELS, 2 *...  7.64 us
    pallas_call x2, Pallas kernels, pack(): pl.pallas_call(functools.partial(pack_kernel, chunk, scaled), out_shape=v...  5.6 us
  transfers between devices with their start and end apart: 6, of which 2 were waited for; matrix products, arithmetic and copies ran while one was open for 0% of the time, Pallas kernels for 12%

profile of v4, /device:TPU:7, one launch (start us, length us, event | category | flops | bytes accessed | tf_op | source)
XLA Modules:
  0.0 117.9 jit_solution(13707205390630160848)
XLA Ops:
  0.6 2.9 %pack_one.1 = f32[16,13,8,128]{3,2,1,0:T(8,128)} custom-call(s32[1]{0:T(128)} %bitcast.2.last_ref, f32[4,8,1536]{2,1,0:T(8,128)} %refs_0_.3, f32[4,8,1536]{2,1,0:T(8,128)} %refs_1_.2, f32[4,8,1536]{2,1,0:T(8,128)} %refs_2_.2, f32[4,8,1536]{2,1,0:T(8,128)} %refs_3_.2), custom_call_target="tpu_custom_call" | custom-call | flops 1000000 | bytes 4194304 | tf_op jit(solution)/shard_map/pack_one/pallas_call | solution.py:102
  3.6 7.8 %all-to-all-start = ((f32[16,13,8,128]{3,2,1,0:T(8,128)}), f32[16,13,8,128]{3,2,1,0:T(8,128)S(1)}, u32[]{:S(2)}, u32[]{:S(2)}) async-start(f32[16,13,8,128]{3,2,1,0:T(8,128)} %pack_one.1), calls=%async_computation | async-start | bytes 1703936 | tf_op jit(solution)/shard_map/all_to_all | solution.py:435
  11.4 2.7 %pack_all.1 = f32[16,10,8,128]{3,2,1,0:T(8,128)} custom-call(s32[1]{0:T(128)} %bitcast.2.last_ref, f32[4,8,1536]{2,1,0:T(8,128)} %refs_0_.3, f32[4,8,1536]{2,1,0:T(8,128)} %refs_1_.3, f32[4,8,1536]{2,1,0:T(8,128)} %refs_2_.3, f32[4,8,1536]{2,1,0:T(8,128)} %refs_3_.3), custom_call_target="tpu_custom_call" | custom-call | flops 1000000 | bytes 4194304 | tf_op jit(solution)/shard_map/pack_all/pallas_call | solution.py:102
  14.0 21.4 %all-to-all-done.x_ref = f32[16,13,8,128]{3,2,1,0:T(8,128)S(1)} async-done(((f32[16,13,8,128]{3,2,1,0:T(8,128)}), f32[16,13,8,128]{3,2,1,0:T(8,128)S(1)}, u32[]{:S(2)}, u32[]{:S(2)}) %all-to-all-start) | async-done | bytes 852000 | tf_op jit(solution)/shard_map/all_to_all | solution.py:435
  35.4 3.5 %all-to-all-start.1 = ((f32[16,10,8,128]{3,2,1,0:T(8,128)}), f32[16,10,8,128]{3,2,1,0:T(8,128)S(1)}, u32[]{:S(2)}, u32[]{:S(2)}) async-start(f32[16,10,8,128]{3,2,1,0:T(8,128)} %pack_all.1), calls=%async_computation.1 | async-start | bytes 1310720 | tf_op jit(solution)/shard_map/all_to_all | solution.py:435
  38.9 0.1 pad_add_fusion.gap_ref
  39.0 1.8 %edges.2 = (f32[2,64,8,128]{3,2,1,0:T(8,128)S(1)}, f32[2,64,8,128]{3,2,1,0:T(8,128)S(1)}, f32[4,8,24,128]{3,2,1,0:T(8,128)S(1)}, f32[4,8,24,128]{3,2,1,0:T(8,128)S(1)}) custom-call(s32[2]{0:T(128)S(1)} %pad_add_fusion.gap_ref, f32[16,13,8,128]{3,2,1,0:T(8,128)S(1)} %all-to-all-done.x_ref), custom_call_target="tpu_custom_call" | custom-call | tf_op jit(solution)/shard_map/edges/pallas_call | solution.py:151
  40.8 4.0 %collective-permute-start = (f32[4,8,24,128]{3,2,1,0:T(8,128)S(1)}, f32[4,8,24,128]{3,2,1,0:T(8,128)S(1)}, u32[]{:S(2)}, u32[]{:S(2)}) collective-permute-start(f32[4,8,24,128]{3,2,1,0:T(8,128)S(1)} %get-tuple-element.21), channel_id=1, source_target_pairs={{0,16},{32,48},{64,80},{96,112},{128,144},{160,176},{192,208},{224... | collective-permute-start | bytes 1179656 | tf_op jit(solution)/shard_map/ppermute | solution.py:438
  44.8 9.1 %collective-permute-start.1 = (f32[4,8,24,128]{3,2,1,0:T(8,128)S(1)}, f32[4,8,24,128]{3,2,1,0:T(8,128)S(1)}, u32[]{:S(2)}, u32[]{:S(2)}) collective-permute-start(f32[4,8,24,128]{3,2,1,0:T(8,128)S(1)} %get-tuple-element.22), channel_id=1, source_target_pairs={{16,32},{48,64},{80,96},{112,128},{144,160},{176,192},{208,224},{2... | collective-permute-start | bytes 1179656 | tf_op jit(solution)/shard_map/ppermute | solution.py:438
  53.9 4.6 %all-to-all-done.1.x_ref = f32[16,10,8,128]{3,2,1,0:T(8,128)S(1)} async-done(((f32[16,10,8,128]{3,2,1,0:T(8,128)}), f32[16,10,8,128]{3,2,1,0:T(8,128)S(1)}, u32[]{:S(2)}, u32[]{:S(2)}) %all-to-all-start.1) | async-done | bytes 655392 | tf_op jit(solution)/shard_map/all_to_all | solution.py:435
  58.6 1.7 %edges.3 = (f32[3,64,8,128]{3,2,1,0:T(8,128)S(1)}, f32[3,8,24,128]{3,2,1,0:T(8,128)S(1)}, f32[3,8,24,128]{3,2,1,0:T(8,128)S(1)}) custom-call(s32[2]{0:T(128)S(1)} %pad_add_fusion.gap_ref, f32[16,10,8,128]{3,2,1,0:T(8,128)S(1)} %all-to-all-done.1.x_ref), custom_call_target="tpu_custom_call" | custom-call | tf_op jit(solution)/shard_map/edges/pallas_call | solution.py:151
  60.2 4.0 %collective-permute-start.2 = (f32[3,8,24,128]{3,2,1,0:T(8,128)S(1)}, f32[3,8,24,128]{3,2,1,0:T(8,128)S(1)}, u32[]{:S(2)}, u32[]{:S(2)}) collective-permute-start(f32[3,8,24,128]{3,2,1,0:T(8,128)S(1)} %get-tuple-element.27), channel_id=1, source_target_pairs={{0,16},{32,48},{64,80},{96,112},{128,144},{160,176},{192,208},{224... | collective-permute-start | bytes 884744 | tf_op jit(solution)/shard_map/ppermute | solution.py:438
  64.2 9.1 %collective-permute-start.3 = (f32[3,8,24,128]{3,2,1,0:T(8,128)S(1)}, f32[3,8,24,128]{3,2,1,0:T(8,128)S(1)}, u32[]{:S(2)}, u32[]{:S(2)}) collective-permute-start(f32[3,8,24,128]{3,2,1,0:T(8,128)S(1)} %get-tuple-element.28), channel_id=1, source_target_pairs={{16,32},{48,64},{80,96},{112,128},{144,160},{176,192},{208,224},{2... | collective-permute-start | bytes 884744 | tf_op jit(solution)/shard_map/ppermute | solution.py:438
  73.4 0.0 collective-permute-done.first_ref
  73.4 0.0 collective-permute-done.1.second_ref
  73.4 7.6 %first_columns.1 = (f32[16,3,8,128]{3,2,1,0:T(8,128)S(1)}, f32[64,6,8,128]{3,2,1,0:T(8,128)S(1)}, f32[2,64,8,128]{3,2,1,0:T(8,128)S(1)}, f32[64,8,128]{2,1,0:T(8...) custom-call(s32[2]{0:T(128)S(1)} %pad_add_fusion.gap_ref, ...), custom_call_target="tpu_custom_call" | custom-call | tf_op jit(solution)/shard_map/first_columns/pallas_call | solution.py:306
  81.0 0.0 collective-permute-done.2.first_ref
  81.0 0.0 collective-permute-done.3.second_ref
  81.0 8.1 %second_columns.1 = f32[16,13,8,128]{3,2,1,0:T(8,128)S(1)} custom-call(s32[2]{0:T(128)S(1)} %pad_add_fusion.gap_ref, s32[16]{0:T(128)S(1)} %get-tuple-element.23.bound_ref, f32[3,64,8,128]{3,2,1,0:T(8,128)S(1)} %get-tuple-element.24.x_ref, f32[2,64,8,128]{3,2,1,0:T(8,128)S(1)} %get-tuple-element.20.c_ref, ...), custom_call_target="tpu_custom_call" | custom-call | tf_op jit(solution)/shard_map/second_columns/pallas_call | solution.py:373
  89.1 27.6 %all_to_all.15.x_ref = f32[16,13,8,128]{3,2,1,0:T(8,128)S(1)} all-to-all(f32[16,13,8,128]{3,2,1,0:T(8,128)S(1)} %second_columns.1), channel_id=1, replica_groups=mesh['lat'=32,'lev'=16] {'lev'}, dimensions={0} | all-to-all | bytes 1703936 | tf_op jit(solution)/shard_map/all_to_all | solution.py:435
  116.7 1.1 unpack.1
Async XLA Ops:
  3.6 31.8 %all-to-all-start = ((f32[16,13,8,128]{3,2,1,0:T(8,128)}), f32[16,13,8,128]{3,2,1,0:T(8,128)S(1)}, u32[]{:S(2)}, u32[]{:S(2)}) async-start(f32[16,13,8,128]{3,2,1,0:T(8,128)} %pack_one.1), calls=%async_computation | async-start | bytes 1703936 | tf_op jit(solution)/shard_map/all_to_all | solution.py:435
  35.4 23.2 %all-to-all-start.1 = ((f32[16,10,8,128]{3,2,1,0:T(8,128)}), f32[16,10,8,128]{3,2,1,0:T(8,128)S(1)}, u32[]{:S(2)}, u32[]{:S(2)}) async-start(f32[16,10,8,128]{3,2,1,0:T(8,128)} %pack_all.1), calls=%async_computation.1 | async-start | bytes 1310720 | tf_op jit(solution)/shard_map/all_to_all | solution.py:435
  40.8 32.6 %collective-permute-start = (f32[4,8,24,128]{3,2,1,0:T(8,128)S(1)}, f32[4,8,24,128]{3,2,1,0:T(8,128)S(1)}, u32[]{:S(2)}, u32[]{:S(2)}) collective-permute-start(f32[4,8,24,128]{3,2,1,0:T(8,128)S(1)} %get-tuple-element.21), channel_id=1, source_target_pairs={{0,16},{32,48},{64,80},{96,112},{128,144},{160,176},{192,208},{224... | collective-permute-start | bytes 1179656 | tf_op jit(solution)/shard_map/ppermute | solution.py:438
  44.8 28.6 %collective-permute-start.1 = (f32[4,8,24,128]{3,2,1,0:T(8,128)S(1)}, f32[4,8,24,128]{3,2,1,0:T(8,128)S(1)}, u32[]{:S(2)}, u32[]{:S(2)}) collective-permute-start(f32[4,8,24,128]{3,2,1,0:T(8,128)S(1)} %get-tuple-element.22), channel_id=1, source_target_pairs={{16,32},{48,64},{80,96},{112,128},{144,160},{176,192},{208,224},{2... | collective-permute-start | bytes 1179656 | tf_op jit(solution)/shard_map/ppermute | solution.py:438
  60.2 20.8 %collective-permute-start.2 = (f32[3,8,24,128]{3,2,1,0:T(8,128)S(1)}, f32[3,8,24,128]{3,2,1,0:T(8,128)S(1)}, u32[]{:S(2)}, u32[]{:S(2)}) collective-permute-start(f32[3,8,24,128]{3,2,1,0:T(8,128)S(1)} %get-tuple-element.27), channel_id=1, source_target_pairs={{0,16},{32,48},{64,80},{96,112},{128,144},{160,176},{192,208},{224... | collective-permute-start | bytes 884744 | tf_op jit(solution)/shard_map/ppermute | solution.py:438
  64.2 16.8 %collective-permute-start.3 = (f32[3,8,24,128]{3,2,1,0:T(8,128)S(1)}, f32[3,8,24,128]{3,2,1,0:T(8,128)S(1)}, u32[]{:S(2)}, u32[]{:S(2)}) collective-permute-start(f32[3,8,24,128]{3,2,1,0:T(8,128)S(1)} %get-tuple-element.28), channel_id=1, source_target_pairs={{16,32},{48,64},{80,96},{112,128},{144,160},{176,192},{208,224},{2... | collective-permute-start | bytes 884744 | tf_op jit(solution)/shard_map/ppermute | solution.py:438

commit v5 on v4

--- a/solution.py
+++ b/solution.py
@@ -110,16 +110,26 @@
     )(last, *(pltpu.with_memory_space_constraint(x, pltpu.HBM) for x in args))
 
 
+def in_order(even, act, refs):
+    first_ref, second_ref = refs[-2:]
+
+    @pl.when(even)
+    def _():
+        act(first_ref, second_ref)
+
+    @pl.when(jnp.logical_not(even))
+    def _():
+        act(second_ref, first_ref)
+
+
 def edges_kernel(chunk, outs, gap_ref, x_ref, *refs):
-    first_ref, second_ref = refs[-2:]
-    even = gap_ref[1] > 0
     out_refs = [ref.at[k] for ref, n in zip(refs[:-2], outs) for k in range(n)]
     where = places(chunk)
-    gap = gap_ref[0]
+    gap = gap_ref[0] % 4
     rel = (iota(1) - gap * SPARE + LANES) % LANES
     quarter = rel // SPARE
 
-    def group(g, _):
+    def group(north_ref, south_ref, g, _):
         for half in range(2):
             src = 2 * g + half
             sides = x_ref[src, 3 * len(chunk)]
@@ -138,12 +148,11 @@
                     x = jnp.where(in_west, turn(sides, SPARE - west - at_west), x)
                     i = OWN * half + l
                     out_refs[f][OWN * src + l] = x
-                    north = pltpu.roll(x, 3, 0)
-                    first_ref[f, g, 3 * i : 3 * i + 3, :] = jnp.where(even, north, x)[0:3]
-                    second_ref[f, g, 3 * i : 3 * i + 3, :] = jnp.where(even, x, north)[0:3]
+                    north_ref[f, g, 3 * i : 3 * i + 3, :] = x[5:8]
+                    south_ref[f, g, 3 * i : 3 * i + 3, :] = x[0:3]
         return 0
 
-    lax.fori_loop(0, 8, group, 0)
+    in_order(gap_ref[0] >= 4, lambda north, south: lax.fori_loop(0, 8, functools.partial(group, north, south), 0), refs)
 
 
 def edges(chunk, outs, gap, x):
@@ -162,15 +171,15 @@
     for f, halo in enumerate(halo_refs):
         halo[...] = jnp.zeros(halo.shape, jnp.float32)
 
-    def group(g, _):
+    def group(north_ref, south_ref, g, _):
         for f, halo in enumerate(halo_refs):
             for i in range(8):
-                a, b = (ref[f, g, 3 * i : 3 * i + 3, :] for ref in (first_ref, second_ref))
-                halo[8 * g + i, 0:3, :] = jnp.where(even, a, b)
-                halo[8 * g + i, 5:8, :] = jnp.where(even, b, a)
+                halo[8 * g + i, 0:3, :] = north_ref[f, g, 3 * i : 3 * i + 3, :]
+                halo[8 * g + i, 5:8, :] = south_ref[f, g, 3 * i : 3 * i + 3, :]
         return 0
 
-    lax.fori_loop(0, 8, group, 0)
+    act = lambda north, south: lax.fori_loop(0, 8, functools.partial(group, north, south), 0)
+    in_order(even, act, (first_ref, second_ref))
 
 
 def shifted(pair, by, edge):
@@ -247,9 +256,9 @@
     out_ref, push_ref, halo_c_ref, top, inverse, h_ref, bound_ref,
     halo_x, final, prefix, least, most,
 ):
-    gap = gap_ref[0]
+    gap = gap_ref[0] % 4
     is_top, is_bottom = iota(0) == ROWS - 1, iota(0) == 0
-    join_strips(gap_ref[1] > 0, first_ref, second_ref, [halo_x.at[0], halo_x.at[1], halo_c_ref.at[0], halo_c_ref.at[1]])
+    join_strips(gap_ref[0] >= 4, first_ref, second_ref, [halo_x.at[0], halo_x.at[1], halo_c_ref.at[0], halo_c_ref.at[1]])
 
     def group(g, carried):
         prefix[0, g] = carried[-1]
@@ -332,9 +341,9 @@
     gap_ref, bound_ref, x_ref, c_ref, halo_c_ref, push_ref, first_ref, second_ref, top, inverse, h_ref, theta_ref,
     out_ref, halo, final, prefix,
 ):
-    gap = gap_ref[0]
+    gap = gap_ref[0] % 4
     is_top, is_bottom = iota(0) == ROWS - 1, iota(0) == 0
-    join_strips(gap_ref[1] > 0, first_ref, second_ref, [halo.at[f] for f in range(3)])
+    join_strips(gap_ref[0] >= 4, first_ref, second_ref, [halo.at[f] for f in range(3)])
 
     def group(g, carried):
         for f in range(3):
@@ -427,7 +436,7 @@
 def body(dp, u, v, th, tr, cn, ce):
     lats = lax.axis_size("lat")
     last = (lax.axis_index("lat") == lats - 1).astype(jnp.int32).reshape(1)
-    gap = jnp.stack([(3 * lax.axis_index("lev") + 3) % 4, 1 - lax.axis_index("lat") % 2]).astype(jnp.int32)
+    gap = ((3 * lax.axis_index("lev") + 3) % 4 + 4 * (1 - lax.axis_index("lat") % 2)).astype(jnp.int32).reshape(1)
     swaps = [[(i, i + 1) for i in range(start, lats - 1, 2)] for start in (0, 1)]
     swaps = [pairs + [(b, a) for a, b in pairs] for pairs in swaps]
 

time: 118 us -> 117 us (level)
  Pallas kernels: 25.9 us -> 24.3 us
  transfers between devices with their start and end apart: 6 -> 6, of which waited for: 2 -> 2; matrix products, arithmetic and copies ran while one was open for 0% -> 0% of each run, Pallas kernels for 12% -> 10%
where the time goes in v5:
time: 117 us
  starting transfers between devices  37.5 us (32%)
  blocking collectives  27.6 us (24%)
  waiting for transfers between devices  26.6 us (23%)
  Pallas kernels  24.3 us (21%)
    all_to_all x1, blocking collectives, across(): return lax.all_to_all(x, 'lev', 0, 0, tiled=True)  27.6 us
    all_to_all x2, waiting for transfers between devices, across(): return lax.all_to_all(x, 'lev', 0, 0, tiled=True)  26.6 us
    ppermute x2, starting transfers between devices, strips(): lax.ppermute(second, 'lat', swaps[1])  18.2 us
    all_to_all x2, starting transfers between devices, across(): return lax.all_to_all(x, 'lev', 0, 0, tiled=True)  11.3 us
    pallas_call x1, Pallas kernels, second_columns(): pl.pallas_call(second_kernel, out_shape=vmem(GROUP, 13), in_specs=[IN_SME...  8.09 us
    ppermute x2, starting transfers between devices, strips(): lax.ppermute(first, 'lat', swaps[0])  7.99 us
    pallas_call x1, Pallas kernels, first_columns(): pl.pallas_call(first_kernel, out_shape=(vmem(GROUP, 3), vmem(LEVELS, 2 *...  7.1 us
    pallas_call x2, Pallas kernels, pack(): pl.pallas_call(functools.partial(pack_kernel, chunk, scaled), out_shape=v...  5.6 us
  transfers between devices with their start and end apart: 6, of which 2 were waited for; matrix products, arithmetic and copies ran while one was open for 0% of the time, Pallas kernels for 10%

profile of v5, /device:TPU:7, one launch (start us, length us, event | category | flops | bytes accessed | tf_op | source)
XLA Modules:
  0.0 116.8 jit_solution(3211263635295039739)
XLA Ops:
  0.6 2.9 %pack_one.1 = f32[16,13,8,128]{3,2,1,0:T(8,128)} custom-call(s32[1]{0:T(128)} %bitcast.1.last_ref, f32[4,8,1536]{2,1,0:T(8,128)} %refs_0_.3, f32[4,8,1536]{2,1,0:T(8,128)} %refs_1_.2, f32[4,8,1536]{2,1,0:T(8,128)} %refs_2_.2, f32[4,8,1536]{2,1,0:T(8,128)} %refs_3_.2), custom_call_target="tpu_custom_call" | custom-call | flops 1000000 | bytes 4194304 | tf_op jit(solution)/shard_map/pack_one/pallas_call | solution.py:102
  3.6 7.8 %all-to-all-start = ((f32[16,13,8,128]{3,2,1,0:T(8,128)}), f32[16,13,8,128]{3,2,1,0:T(8,128)S(1)}, u32[]{:S(2)}, u32[]{:S(2)}) async-start(f32[16,13,8,128]{3,2,1,0:T(8,128)} %pack_one.1), calls=%async_computation | async-start | bytes 1703936 | tf_op jit(solution)/shard_map/all_to_all | solution.py:444
  11.4 2.7 %pack_all.1 = f32[16,10,8,128]{3,2,1,0:T(8,128)} custom-call(s32[1]{0:T(128)} %bitcast.1.last_ref, f32[4,8,1536]{2,1,0:T(8,128)} %refs_0_.3, f32[4,8,1536]{2,1,0:T(8,128)} %refs_1_.3, f32[4,8,1536]{2,1,0:T(8,128)} %refs_2_.3, f32[4,8,1536]{2,1,0:T(8,128)} %refs_3_.3), custom_call_target="tpu_custom_call" | custom-call | flops 1000000 | bytes 4194304 | tf_op jit(solution)/shard_map/pack_all/pallas_call | solution.py:102
  14.0 21.4 %all-to-all-done.x_ref = f32[16,13,8,128]{3,2,1,0:T(8,128)S(1)} async-done(((f32[16,13,8,128]{3,2,1,0:T(8,128)}), f32[16,13,8,128]{3,2,1,0:T(8,128)S(1)}, u32[]{:S(2)}, u32[]{:S(2)}) %all-to-all-start) | async-done | bytes 852000 | tf_op jit(solution)/shard_map/all_to_all | solution.py:444
  35.4 3.5 %all-to-all-start.1 = ((f32[16,10,8,128]{3,2,1,0:T(8,128)}), f32[16,10,8,128]{3,2,1,0:T(8,128)S(1)}, u32[]{:S(2)}, u32[]{:S(2)}) async-start(f32[16,10,8,128]{3,2,1,0:T(8,128)} %pack_all.1), calls=%async_computation.1 | async-start | bytes 1310720 | tf_op jit(solution)/shard_map/all_to_all | solution.py:444
  38.9 1.3 %edges.2 = (f32[2,64,8,128]{3,2,1,0:T(8,128)S(1)}, f32[2,64,8,128]{3,2,1,0:T(8,128)S(1)}, f32[4,8,24,128]{3,2,1,0:T(8,128)S(1)}, f32[4,8,24,128]{3,2,1,0:T(8,128)S(1)}) custom-call(s32[1]{0:T(128)} %bitcast.gap_ref, f32[16,13,8,128]{3,2,1,0:T(8,128)S(1)} %all-to-all-done.x_ref), custom_call_target="tpu_custom_call" | custom-call | tf_op jit(solution)/shard_map/edges/pallas_call | solution.py:160
  40.2 4.0 %collective-permute-start = (f32[4,8,24,128]{3,2,1,0:T(8,128)S(1)}, f32[4,8,24,128]{3,2,1,0:T(8,128)S(1)}, u32[]{:S(2)}, u32[]{:S(2)}) collective-permute-start(f32[4,8,24,128]{3,2,1,0:T(8,128)S(1)} %get-tuple-element.21), channel_id=1, source_target_pairs={{0,16},{32,48},{64,80},{96,112},{128,144},{160,176},{192,208},{224... | collective-permute-start | bytes 1179656 | tf_op jit(solution)/shard_map/ppermute | solution.py:447
  44.2 9.1 %collective-permute-start.1 = (f32[4,8,24,128]{3,2,1,0:T(8,128)S(1)}, f32[4,8,24,128]{3,2,1,0:T(8,128)S(1)}, u32[]{:S(2)}, u32[]{:S(2)}) collective-permute-start(f32[4,8,24,128]{3,2,1,0:T(8,128)S(1)} %get-tuple-element.22), channel_id=1, source_target_pairs={{16,32},{48,64},{80,96},{112,128},{144,160},{176,192},{208,224},{2... | collective-permute-start | bytes 1179656 | tf_op jit(solution)/shard_map/ppermute | solution.py:447
  53.3 5.2 %all-to-all-done.1.x_ref = f32[16,10,8,128]{3,2,1,0:T(8,128)S(1)} async-done(((f32[16,10,8,128]{3,2,1,0:T(8,128)}), f32[16,10,8,128]{3,2,1,0:T(8,128)S(1)}, u32[]{:S(2)}, u32[]{:S(2)}) %all-to-all-start.1) | async-done | bytes 655392 | tf_op jit(solution)/shard_map/all_to_all | solution.py:444
  58.6 1.1 edges.3
  59.7 4.0 %collective-permute-start.2 = (f32[3,8,24,128]{3,2,1,0:T(8,128)S(1)}, f32[3,8,24,128]{3,2,1,0:T(8,128)S(1)}, u32[]{:S(2)}, u32[]{:S(2)}) collective-permute-start(f32[3,8,24,128]{3,2,1,0:T(8,128)S(1)} %get-tuple-element.27), channel_id=1, source_target_pairs={{0,16},{32,48},{64,80},{96,112},{128,144},{160,176},{192,208},{224... | collective-permute-start | bytes 884744 | tf_op jit(solution)/shard_map/ppermute | solution.py:447
  63.7 9.1 %collective-permute-start.3 = (f32[3,8,24,128]{3,2,1,0:T(8,128)S(1)}, f32[3,8,24,128]{3,2,1,0:T(8,128)S(1)}, u32[]{:S(2)}, u32[]{:S(2)}) collective-permute-start(f32[3,8,24,128]{3,2,1,0:T(8,128)S(1)} %get-tuple-element.28), channel_id=1, source_target_pairs={{16,32},{48,64},{80,96},{112,128},{144,160},{176,192},{208,224},{2... | collective-permute-start | bytes 884744 | tf_op jit(solution)/shard_map/ppermute | solution.py:447
  72.8 0.0 collective-permute-done.first_ref
  72.8 0.0 collective-permute-done.1.second_ref
  72.8 7.1 %first_columns.1 = (f32[16,3,8,128]{3,2,1,0:T(8,128)S(1)}, f32[64,6,8,128]{3,2,1,0:T(8,128)S(1)}, f32[2,64,8,128]{3,2,1,0:T(8,128)S(1)}, f32[64,8,128]{2,1,0:T(8...) custom-call(s32[1]{0:T(128)} %bitcast.gap_ref, ...), custom_call_target="tpu_custom_call" | custom-call | tf_op jit(solution)/shard_map/first_columns/pallas_call | solution.py:315
  79.9 0.0 collective-permute-done.2.first_ref
  79.9 0.0 collective-permute-done.3.second_ref
  80.0 8.1 %second_columns.1 = f32[16,13,8,128]{3,2,1,0:T(8,128)S(1)} custom-call(s32[1]{0:T(128)} %bitcast.gap_ref, s32[16]{0:T(128)S(1)} %get-tuple-element.23.bound_ref, f32[3,64,8,128]{3,2,1,0:T(8,128)S(1)} %get-tuple-element.24.x_ref, f32[2,64,8,128]{3,2,1,0:T(8,128)S(1)} %get-tuple-element.20.c_ref, f32[2,64,8,128]{3,2,1,0:T(8,128)S(1)} %get-tuple-element.25.halo_c_ref, ...), custom_call_target="tpu_custom_call" | custom-call | tf_op jit(solution)/shard_map/second_columns/pallas_call | solution.py:382
  88.1 27.6 %all_to_all.15.x_ref = f32[16,13,8,128]{3,2,1,0:T(8,128)S(1)} all-to-all(f32[16,13,8,128]{3,2,1,0:T(8,128)S(1)} %second_columns.1), channel_id=1, replica_groups=mesh['lat'=32,'lev'=16] {'lev'}, dimensions={0} | all-to-all | bytes 1703936 | tf_op jit(solution)/shard_map/all_to_all | solution.py:444
  115.6 1.1 unpack.1
Async XLA Ops:
  3.6 31.8 %all-to-all-start = ((f32[16,13,8,128]{3,2,1,0:T(8,128)}), f32[16,13,8,128]{3,2,1,0:T(8,128)S(1)}, u32[]{:S(2)}, u32[]{:S(2)}) async-start(f32[16,13,8,128]{3,2,1,0:T(8,128)} %pack_one.1), calls=%async_computation | async-start | bytes 1703936 | tf_op jit(solution)/shard_map/all_to_all | solution.py:444
  35.4 23.2 %all-to-all-start.1 = ((f32[16,10,8,128]{3,2,1,0:T(8,128)}), f32[16,10,8,128]{3,2,1,0:T(8,128)S(1)}, u32[]{:S(2)}, u32[]{:S(2)}) async-start(f32[16,10,8,128]{3,2,1,0:T(8,128)} %pack_all.1), calls=%async_computation.1 | async-start | bytes 1310720 | tf_op jit(solution)/shard_map/all_to_all | solution.py:444
  40.2 32.6 %collective-permute-start = (f32[4,8,24,128]{3,2,1,0:T(8,128)S(1)}, f32[4,8,24,128]{3,2,1,0:T(8,128)S(1)}, u32[]{:S(2)}, u32[]{:S(2)}) collective-permute-start(f32[4,8,24,128]{3,2,1,0:T(8,128)S(1)} %get-tuple-element.21), channel_id=1, source_target_pairs={{0,16},{32,48},{64,80},{96,112},{128,144},{160,176},{192,208},{224... | collective-permute-start | bytes 1179656 | tf_op jit(solution)/shard_map/ppermute | solution.py:447
  44.2 28.6 %collective-permute-start.1 = (f32[4,8,24,128]{3,2,1,0:T(8,128)S(1)}, f32[4,8,24,128]{3,2,1,0:T(8,128)S(1)}, u32[]{:S(2)}, u32[]{:S(2)}) collective-permute-start(f32[4,8,24,128]{3,2,1,0:T(8,128)S(1)} %get-tuple-element.22), channel_id=1, source_target_pairs={{16,32},{48,64},{80,96},{112,128},{144,160},{176,192},{208,224},{2... | collective-permute-start | bytes 1179656 | tf_op jit(solution)/shard_map/ppermute | solution.py:447
  59.7 20.3 %collective-permute-start.2 = (f32[3,8,24,128]{3,2,1,0:T(8,128)S(1)}, f32[3,8,24,128]{3,2,1,0:T(8,128)S(1)}, u32[]{:S(2)}, u32[]{:S(2)}) collective-permute-start(f32[3,8,24,128]{3,2,1,0:T(8,128)S(1)} %get-tuple-element.27), channel_id=1, source_target_pairs={{0,16},{32,48},{64,80},{96,112},{128,144},{160,176},{192,208},{224... | collective-permute-start | bytes 884744 | tf_op jit(solution)/shard_map/ppermute | solution.py:447
  63.7 16.3 %collective-permute-start.3 = (f32[3,8,24,128]{3,2,1,0:T(8,128)S(1)}, f32[3,8,24,128]{3,2,1,0:T(8,128)S(1)}, u32[]{:S(2)}, u32[]{:S(2)}) collective-permute-start(f32[3,8,24,128]{3,2,1,0:T(8,128)S(1)} %get-tuple-element.28), channel_id=1, source_target_pairs={{16,32},{48,64},{80,96},{112,128},{144,160},{176,192},{208,224},{2... | collective-permute-start | bytes 884744 | tf_op jit(solution)/shard_map/ppermute | solution.py:447
